TPU v7x, 32 devices: a whole 2x2x4 slice. The times are simulated.
32 devices in a mesh: contrast: 4 (over y, x), pa: 2 (over core), pb: 4 (over z).
Axes of the slice: x: 2, y: 2, z: 4, core: 2. Of those that a mesh axis runs over, the one named last changes fastest.
Arguments:
- image: float32 [4, 2, 128, 160, 128], P('contrast', None, 'pa', 'pb'), may hold values from -9 to 9
- coil_maps: bfloat16 [4, 2, 128, 160, 128], P(None, None, 'pa', 'pb'), may hold values from -2 to 2
- kspace: bfloat16 [4, 4, 2, 128, 160, 128], P('contrast', None, None, ('pa', 'pb')), may hold values from -4 to 4
- sampling: int32 [4, 128, 160, 128], P('contrast', ('pa', 'pb')), may hold values 0 or 1
- available: int32 [4], P('contrast'), may hold values from 0 to 1, as said below
Outputs:
- image_next: float32 [4, 2, 128, 160, 128], P('contrast', None, 'pa', 'pb')
- misfit: float32 [], replicated
Inputs may be any that keep to these rules, and one draw needn't show every extreme that they name: `available`: at least one contrast is missing, and at most max(1, 1) are.
All inputs are finite; a program needn't handle non-finite values. No bound on the sum of `sampling` on one device may be relied on, other than what follows from the above.
Results may differ from a plain program's by a relative error of at most 0.0003.
Values sent between devices are 32-bit elements; how exact they have to be, the bound alone decides.
A program may use at most 128 MiB of HBM per device.

v0:
```python
import math

import jax
import jax.numpy as jnp
from jax import lax
from jax.sharding import PartitionSpec as P

step_size = 1.0
threshold = 2.5


def complex_table(length, sign_value):
    indices = lax.iota(jnp.int32, length)
    phases = indices[:, None] * indices[None, :] % length
    angles = phases.astype(jnp.float32) * (2.0 * math.pi / length)
    normalize = 1.0 / math.sqrt(length)
    real_part = jnp.cos(angles) * normalize
    imag_part = sign_value * jnp.sin(angles) * normalize
    upper_rows = jnp.stack([real_part, imag_part], axis=1)
    bottom = jnp.stack([-imag_part, real_part], axis=1)
    return jnp.stack([upper_rows, bottom], axis=0)


def contract(pattern, operand, table):
    return jnp.einsum(
        pattern, operand, table, precision=lax.Precision.HIGHEST, preferred_element_type=jnp.float32
    )


def per_device(image, coil_maps, kspace, sampling, available):
    groups_pa = lax.axis_size("pa")
    groups_pb = lax.axis_size("pb")
    pixels = image[0]
    x_rows = pixels.shape[1]
    y_rows = pixels.shape[2]
    depth_size = pixels.shape[3]
    width_x = x_rows * groups_pa
    width_y = y_rows * groups_pb
    plane_size = x_rows * y_rows
    coil_total = coil_maps.shape[0]
    depth_share = kspace.shape[3]
    present = available[0].astype(jnp.float32)
    weight_factor = sampling[0].astype(jnp.float32) * present
    forward_z = complex_table(depth_size, -1.0)
    forward_y = complex_table(width_y, -1.0).reshape(2, groups_pb, y_rows, 2, width_y)
    forward_x = complex_table(width_x, -1.0).reshape(2, groups_pa, x_rows, 2, width_x)
    inverse_z = complex_table(depth_size, 1.0)
    inverse_y = complex_table(width_y, 1.0).reshape(2, width_y, 2, groups_pb, y_rows)
    inverse_x = complex_table(width_x, 1.0).reshape(2, width_x, 2, groups_pa, x_rows)
    grad_re = jnp.zeros(pixels.shape[1:], jnp.float32)
    grad_im = jnp.zeros(pixels.shape[1:], jnp.float32)
    misfit_local = jnp.zeros((), jnp.float32)
    for coil_index in range(coil_total):
        maps_part = coil_maps[coil_index : coil_index + 1]
        one_members = maps_part.shape[0]
        sens_re = maps_part[:, 0].astype(jnp.float32)
        sens_im = maps_part[:, 1].astype(jnp.float32)
        prod_re = sens_re * pixels[0] - sens_im * pixels[1]
        prod_im = sens_re * pixels[1] + sens_im * pixels[0]
        spread = jnp.stack([prod_re, prod_im], axis=1).reshape(
            one_members, 2, plane_size, depth_size
        )
        transformed = contract("bcmz,czdk->dkbm", spread, forward_z)
        portion = lax.all_to_all(
            transformed[None], ("pa", "pb"), split_axis=2, concat_axis=0, tiled=True
        )
        members = portion.shape[3]
        blocks = portion.reshape(groups_pa, groups_pb, 2, depth_share, members, x_rows, y_rows)
        partial_value = contract("aeczbxy,ceyfl->afzbxl", blocks, forward_y)
        fourier_coefficients = contract("afzbxl,faxdk->bdzlk", partial_value, forward_x)
        kspace_residual = weight_factor * (
            fourier_coefficients - kspace[0, coil_index : coil_index + 1].astype(jnp.float32)
        )
        misfit_part = jnp.sum(kspace_residual * kspace_residual)
        one_partial_value = contract("bczlk,ckfax->afzblx", kspace_residual, inverse_x)
        spatial = contract("afzblx,fldey->aedzbxy", one_partial_value, inverse_y)
        sendable = spatial.reshape(groups_pa * groups_pb, 2, depth_share, one_members, plane_size)
        image_part = contract(
            "ckbm,ckdz->bdmz",
            lax.all_to_all(sendable, ("pa", "pb"), split_axis=0, concat_axis=2, tiled=True)[0],
            inverse_z,
        )
        image_part = image_part.reshape(one_members, 2, x_rows, y_rows, depth_size)
        one_grad_re = jnp.sum(sens_re * image_part[:, 0] + sens_im * image_part[:, 1], axis=0)
        one_grad_im = jnp.sum(sens_re * image_part[:, 1] - sens_im * image_part[:, 0], axis=0)
        grad_re = grad_re + one_grad_re
        grad_im = grad_im + one_grad_im
        misfit_local = misfit_local + misfit_part
    moved_re = pixels[0] - step_size * grad_re
    moved_im = pixels[1] - step_size * grad_im
    energy = present * (moved_re * moved_re + moved_im * moved_im)
    energy_total = lax.psum(energy, "contrast")
    norm_value = jnp.sqrt(energy_total)
    factor = jnp.maximum(norm_value - threshold, 0.0) / jnp.maximum(norm_value, threshold)
    misfit_sum = lax.psum(misfit_local, ("contrast", "pa", "pb"))
    shrink = present * factor
    result = jnp.stack([moved_re * shrink, moved_im * shrink], axis=0)[None]
    count_all = (
        lax.axis_size("contrast") * image.shape[0] * coil_total * width_x * width_y * depth_size
    )
    return (result, misfit_sum / (2.0 * count_all))


def solution(mesh):
    return jax.shard_map(
        per_device,
        mesh=mesh,
        in_specs=(
            P("contrast", None, "pa", "pb", None),
            P(None, None, "pa", "pb", None),
            P("contrast", None, None, ("pa", "pb"), None, None),
            P("contrast", ("pa", "pb"), None, None),
            P("contrast"),
        ),
        out_specs=(P("contrast", None, "pa", "pb", None), P()),
        check_vma=False,
    )
```

profile of v0, /device:TPU:0, one launch (start us, length us, event | category | flops | bytes accessed | tf_op | source)
XLA Modules:
  0.0 657.2 jit_solution(11547883388924909470)
XLA Ops:
  8.0 5.1 fusion.81
  19.2 6.8 %all-to-all-start.6 = ((f32[1,2,128,1,2560]{4,1,3,0,2:T(2,128)}), f32[1,2,128,1,2560]{4,1,3,0,2:T(2,128)}, u32[]{:S(2)}, u32[]{:S(2)}) async-start(f32[1,2,128,1,2560]{4,1,3,0,2:T(2,128)} %copy.100), calls=%async_computation.6 | async-start | bytes 5242880 | tf_op jit(solution)/shard_map/all_to_all | solution.py:64
  26.0 4.4 fusion.80
  36.4 49.3 %all-to-all-done.6 = f32[1,2,128,1,2560]{4,1,3,0,2:T(2,128)} async-done(((f32[1,2,128,1,2560]{4,1,3,0,2:T(2,128)}), f32[1,2,128,1,2560]{4,1,3,0,2:T(2,128)}, u32[]{:S(2)}, u32[]{:S(2)}) %all-to-all-start.6) | async-done | bytes 2621472 | tf_op jit(solution)/shard_map/all_to_all | solution.py:64
  89.4 4.2 convolution_bitcast_fusion.7
  97.1 52.0 %all-to-all-done.2 = f32[1,2,128,1,2560]{4,1,3,0,2:T(2,128)S(1)} async-done(((f32[1,2,128,1,2560]{4,1,3,0,2:T(2,128)}), f32[1,2,128,1,2560]{4,1,3,0,2:T(2,128)S(1)}, u32[]{:S(2)}, u32[]{:S(2)}) %all-to-all-start.2) | async-done | bytes 2621472 | tf_op jit(solution)/shard_map/all_to_all | solution.py:64
  150.5 4.6 all-to-all-start
  155.1 4.2 convolution_bitcast_fusion.3
  162.8 52.0 %all-to-all-done = f32[1,2,128,1,2560]{4,1,3,0,2:T(2,128)} async-done(((f32[1,2,128,1,2560]{4,1,3,0,2:T(2,128)}), f32[1,2,128,1,2560]{4,1,3,0,2:T(2,128)}, u32[]{:S(2)}, u32[]{:S(2)}) %all-to-all-start) | async-done | bytes 2621472 | tf_op jit(solution)/shard_map/all_to_all | solution.py:64
  214.9 4.4 all-to-all-start.4
  223.6 3.8 copy.229
  227.4 9.0 %reshape.822 = f32[2,4,2,16,64,40]{5,4,3,2,1,0:T(8,128)} reshape(f32[8,1,2,16,1,2560]{5,3,2,0,4,1:T(8,128)} %bitcast.491) | data formatting | bytes 5242880 | tf_op jit(solution)/shard_map/reshape.8
  236.4 15.3 %fusion.60 = f32[2,2,16,64,160]{4,3,2,0,1:T(8,128)S(1)} fusion(f32[1,4,40,1,160]{4,2,1,0,3:T(8,128)S(1)} %get-tuple-element.24, f32[1,4,40,1,160]{4,2,1,0,3:T(8,128)S(1)} %get-tuple-element.23, f32[1,4,40,1,160]{4,2,1,0,3:T(8,128)S(1)} %get-tuple-element.22, f32[2,4,2,16,64,40]{5,4,3,2,1,0:T(8,128)} %reshape.822), kind=kOutput, calls=%fused_computation.109 | convolution fusion | flops 2516889600 | bytes 5550080 | tf_op jit(solution)/shard_map/aeczbxy,ceyfl->afzbxl/dot_general | solution.py:25
  251.7 8.9 %multiply_reduce_fusion.3 = (f32[]{:T(128)}, f32[1,2,16,160,128]{4,3,2,1,0:T(8,128)S(1)}) fusion(bf16[1,4,2,16,160,128]{5,4,3,2,1,0:T(8,128)(2,1)} %param.7, f32[2,2,16,64,160]{4,3,2,0,1:T(8,128)S(1)} %fusion.60, f32[1,2,64,1,128]{4,2,0,1,3:T(8,128)S(1)} %get-tuple-element.30, f32[1,2,64,1,128]{4,2,0,1,3:T(8,128)S(1)} %get-tuple-element.29, ...), kind=kOutput, calls=%fused_computation.72 | convolution fusion | flops 2016739328 | bytes 8060932 | tf_op jit(solution)/shard_map/afzbxl,faxdk->bdzlk/dot_general | solution.py:25
  264.3 10.3 %fusion.48 = f32[2,4,2,16,1,64,40]{5,6,3,0,1,2,4:T(8,128)} fusion(f32[2,2,64,16,160,1]{4,2,3,5,1,0:T(8,128)S(1)} %fusion.45, f32[1,160,1,4,40]{1,4,0,3,2:T(8,128)S(1)} %get-tuple-element.21, f32[1,160,1,4,40]{1,4,0,3,2:T(8,128)S(1)} %get-tuple-element.20, f32[1,160,1,4,40]{1,4,0,3,2:T(8,128)S(1)} %get-tuple-element.19), kind=kOutput, calls=%fused_computation.73 | convolution fusion | flops 2516889600 | bytes 5550080 | tf_op jit(solution)/shard_map/afzblx,fldey->aedzbxy/dot_general | solution.py:25
  274.6 7.9 %copy.76 = f32[2,4,2,16,1,64,40]{6,5,3,2,1,0,4:T(8,128)} copy(f32[2,4,2,16,1,64,40]{5,6,3,0,1,2,4:T(8,128)} %fusion.48) | data formatting | bytes 5242880 | tf_op jit(solution)/shard_map/afzblx,fldey->aedzbxy/transpose | solution.py:25
  282.5 8.1 %reshape.826 = f32[8,2,16,1,2560]{4,2,1,0,3:T(8,128)} reshape(f32[2,4,2,16,1,64,40]{6,5,3,2,1,0,4:T(8,128)} %copy.76) | data formatting | bytes 5242880 | tf_op jit(solution)/shard_map/reshape | solution.py:77
  290.6 5.2 all-to-all-start.1
  299.6 9.0 %reshape.838 = f32[2,4,2,16,64,40]{5,4,3,2,1,0:T(8,128)} reshape(f32[8,1,2,16,1,2560]{5,3,2,0,4,1:T(8,128)} %bitcast.492) | data formatting | bytes 5242880 | tf_op jit(solution)/shard_map/reshape.63
  308.6 15.2 %fusion.66 = f32[2,2,16,64,160]{4,3,2,0,1:T(8,128)S(1)} fusion(f32[1,4,40,1,160]{4,2,1,0,3:T(8,128)S(1)} %get-tuple-element.24, f32[1,4,40,1,160]{4,2,1,0,3:T(8,128)S(1)} %get-tuple-element.23, f32[1,4,40,1,160]{4,2,1,0,3:T(8,128)S(1)} %get-tuple-element.22, f32[2,4,2,16,64,40]{5,4,3,2,1,0:T(8,128)} %reshape.838), kind=kOutput, calls=%fused_computation.111 | convolution fusion | flops 2516889600 | bytes 5550080 | tf_op jit(solution)/shard_map/aeczbxy,ceyfl->afzbxl/dot_general | solution.py:25
  323.7 8.9 %multiply_reduce_fusion.1 = (f32[]{:T(128)}, f32[1,2,16,160,128]{4,3,2,1,0:T(8,128)S(1)}) fusion(bf16[1,4,2,16,160,128]{5,4,3,2,1,0:T(8,128)(2,1)} %param.7, f32[2,2,16,64,160]{4,3,2,0,1:T(8,128)S(1)} %fusion.66, f32[1,2,64,1,128]{4,2,0,1,3:T(8,128)S(1)} %get-tuple-element.30, f32[1,2,64,1,128]{4,2,0,1,3:T(8,128)S(1)} %get-tuple-element.29, ...), kind=kOutput, calls=%fused_computation.70 | convolution fusion | flops 2016739328 | bytes 8060932 | tf_op jit(solution)/shard_map/afzbxl,faxdk->bdzlk/dot_general | solution.py:25
  336.4 10.6 %fusion.54 = f32[2,4,2,16,1,64,40]{5,6,3,0,1,2,4:T(8,128)} fusion(f32[2,2,64,16,160,1]{4,2,3,5,1,0:T(8,128)S(1)} %fusion.39, f32[1,160,1,4,40]{1,4,0,3,2:T(8,128)S(1)} %get-tuple-element.21, f32[1,160,1,4,40]{1,4,0,3,2:T(8,128)S(1)} %get-tuple-element.20, f32[1,160,1,4,40]{1,4,0,3,2:T(8,128)S(1)} %get-tuple-element.19), kind=kOutput, calls=%fused_computation.75 | convolution fusion | flops 2516889600 | bytes 5550080 | tf_op jit(solution)/shard_map/afzblx,fldey->aedzbxy/dot_general | solution.py:25
  347.0 7.9 %copy.96 = f32[2,4,2,16,1,64,40]{6,5,3,2,1,0,4:T(8,128)} copy(f32[2,4,2,16,1,64,40]{5,6,3,0,1,2,4:T(8,128)} %fusion.54) | data formatting | bytes 5242880 | tf_op jit(solution)/shard_map/afzblx,fldey->aedzbxy/transpose | solution.py:25
  354.9 8.1 %reshape.842 = f32[8,2,16,1,2560]{4,2,1,0,3:T(8,128)} reshape(f32[2,4,2,16,1,64,40]{6,5,3,2,1,0,4:T(8,128)} %copy.96) | data formatting | bytes 5242880 | tf_op jit(solution)/shard_map/reshape | solution.py:77
  363.0 5.3 all-to-all-start.5
  368.3 3.8 copy.228
  372.1 9.0 %reshape.830 = f32[2,4,2,16,64,40]{5,4,3,2,1,0:T(8,128)} reshape(f32[8,1,2,16,1,2560]{5,3,2,0,4,1:T(8,128)} %bitcast.493) | data formatting | bytes 5242880 | tf_op jit(solution)/shard_map/reshape.47
  381.1 15.1 %fusion.63 = f32[2,2,16,64,160]{4,3,2,0,1:T(8,128)S(1)} fusion(f32[1,4,40,1,160]{4,2,1,0,3:T(8,128)S(1)} %get-tuple-element.24, f32[1,4,40,1,160]{4,2,1,0,3:T(8,128)S(1)} %get-tuple-element.23, f32[1,4,40,1,160]{4,2,1,0,3:T(8,128)S(1)} %get-tuple-element.22, f32[2,4,2,16,64,40]{5,4,3,2,1,0:T(8,128)} %reshape.830), kind=kOutput, calls=%fused_computation.110 | convolution fusion | flops 2516889600 | bytes 5550080 | tf_op jit(solution)/shard_map/aeczbxy,ceyfl->afzbxl/dot_general | solution.py:25
  396.2 8.8 %multiply_reduce_fusion.2 = (f32[]{:T(128)}, f32[1,2,16,160,128]{4,3,2,1,0:T(8,128)S(1)}) fusion(bf16[1,4,2,16,160,128]{5,4,3,2,1,0:T(8,128)(2,1)} %param.7, f32[2,2,16,64,160]{4,3,2,0,1:T(8,128)S(1)} %fusion.63, f32[1,2,64,1,128]{4,2,0,1,3:T(8,128)S(1)} %get-tuple-element.30, f32[1,2,64,1,128]{4,2,0,1,3:T(8,128)S(1)} %get-tuple-element.29, ...), kind=kOutput, calls=%fused_computation.71 | convolution fusion | flops 2016739328 | bytes 8060932 | tf_op jit(solution)/shard_map/afzbxl,faxdk->bdzlk/dot_general | solution.py:25
  408.7 10.4 %fusion.51 = f32[2,4,2,16,1,64,40]{5,6,3,0,1,2,4:T(8,128)} fusion(f32[2,2,64,16,160,1]{4,2,3,5,1,0:T(8,128)S(1)} %fusion.42, f32[1,160,1,4,40]{1,4,0,3,2:T(8,128)S(1)} %get-tuple-element.21, f32[1,160,1,4,40]{1,4,0,3,2:T(8,128)S(1)} %get-tuple-element.20, f32[1,160,1,4,40]{1,4,0,3,2:T(8,128)S(1)} %get-tuple-element.19), kind=kOutput, calls=%fused_computation.74 | convolution fusion | flops 2516889600 | bytes 5550080 | tf_op jit(solution)/shard_map/afzblx,fldey->aedzbxy/dot_general | solution.py:25
  419.2 7.9 %copy.86 = f32[2,4,2,16,1,64,40]{6,5,3,2,1,0,4:T(8,128)} copy(f32[2,4,2,16,1,64,40]{5,6,3,0,1,2,4:T(8,128)} %fusion.51) | data formatting | bytes 5242880 | tf_op jit(solution)/shard_map/afzblx,fldey->aedzbxy/transpose | solution.py:25
  427.1 8.1 %reshape.834 = f32[8,2,16,1,2560]{4,2,1,0,3:T(8,128)} reshape(f32[2,4,2,16,1,64,40]{6,5,3,2,1,0,4:T(8,128)} %copy.86) | data formatting | bytes 5242880 | tf_op jit(solution)/shard_map/reshape | solution.py:77
  435.2 5.6 all-to-all-start.3
  444.5 9.0 %reshape.846 = f32[2,4,2,16,64,40]{5,4,3,2,1,0:T(8,128)} reshape(f32[8,1,2,16,1,2560]{5,3,2,0,4,1:T(8,128)} %bitcast.494) | data formatting | bytes 5242880 | tf_op jit(solution)/shard_map/reshape.79
  453.5 15.1 %fusion.69 = f32[2,2,16,64,160]{4,3,2,0,1:T(8,128)S(1)} fusion(f32[1,4,40,1,160]{4,2,1,0,3:T(8,128)S(1)} %get-tuple-element.24, f32[1,4,40,1,160]{4,2,1,0,3:T(8,128)S(1)} %get-tuple-element.23, f32[1,4,40,1,160]{4,2,1,0,3:T(8,128)S(1)} %get-tuple-element.22, f32[2,4,2,16,64,40]{5,4,3,2,1,0:T(8,128)} %reshape.846), kind=kOutput, calls=%fused_computation.112 | convolution fusion | flops 2516889600 | bytes 5550080 | tf_op jit(solution)/shard_map/aeczbxy,ceyfl->afzbxl/dot_general | solution.py:25
  468.6 8.9 %multiply_reduce_fusion = (f32[]{:T(128)}, f32[1,2,16,160,128]{4,3,2,1,0:T(8,128)S(1)}) fusion(bf16[1,4,2,16,160,128]{5,4,3,2,1,0:T(8,128)(2,1)} %param.7, f32[2,2,16,64,160]{4,3,2,0,1:T(8,128)S(1)} %fusion.69, f32[1,2,64,1,128]{4,2,0,1,3:T(8,128)S(1)} %get-tuple-element.30, f32[1,2,64,1,128]{4,2,0,1,3:T(8,128)S(1)} %get-tuple-element.29, ...), kind=kOutput, calls=%fused_computation.69 | convolution fusion | flops 2016739328 | bytes 8060932 | tf_op jit(solution)/shard_map/afzbxl,faxdk->bdzlk/dot_general | solution.py:25
  481.1 10.4 %fusion.57 = f32[2,4,2,16,1,64,40]{5,6,3,0,1,2,4:T(8,128)} fusion(f32[2,2,64,16,160,1]{4,2,3,5,1,0:T(8,128)S(1)} %fusion.36, f32[1,160,1,4,40]{1,4,0,3,2:T(8,128)S(1)} %get-tuple-element.21, f32[1,160,1,4,40]{1,4,0,3,2:T(8,128)S(1)} %get-tuple-element.20, f32[1,160,1,4,40]{1,4,0,3,2:T(8,128)S(1)} %get-tuple-element.19), kind=kOutput, calls=%fused_computation.76 | convolution fusion | flops 2516889600 | bytes 5550080 | tf_op jit(solution)/shard_map/afzblx,fldey->aedzbxy/dot_general | solution.py:25
  491.5 7.9 %copy.106 = f32[2,4,2,16,1,64,40]{6,5,3,2,1,0,4:T(8,128)} copy(f32[2,4,2,16,1,64,40]{5,6,3,0,1,2,4:T(8,128)} %fusion.57) | data formatting | bytes 5242880 | tf_op jit(solution)/shard_map/afzblx,fldey->aedzbxy/transpose | solution.py:25
  499.4 8.1 %reshape.850 = f32[8,2,16,1,2560]{4,2,1,0,3:T(8,128)} reshape(f32[2,4,2,16,1,64,40]{6,5,3,2,1,0,4:T(8,128)} %copy.106) | data formatting | bytes 5242880 | tf_op jit(solution)/shard_map/reshape | solution.py:77
  507.5 5.1 all-to-all-start.7
  514.6 3.9 convolution_bitcast_fusion.6
  523.9 3.8 convolution_bitcast_fusion.2
  532.9 4.0 convolution_bitcast_fusion.4
  540.0 32.3 %all-to-all-done.7 = f32[8,2,16,1,2560]{4,2,1,3,0:T(8,128)S(1)} async-done(((f32[8,2,16,1,2560]{4,2,1,3,0:T(8,128)}), f32[8,2,16,1,2560]{4,2,1,3,0:T(8,128)S(1)}, u32[]{:S(2)}, u32[]{:S(2)}) %all-to-all-start.7) | async-done | bytes 2621472 | tf_op jit(solution)/shard_map/all_to_all | solution.py:80
  572.5 3.9 convolution_bitcast_fusion
  579.8 8.4 %add_multiply_fusion = (f32[64,40,128]{2,1,0:T(8,128)}, f32[64,40,128]{2,1,0:T(8,128)}, f32[64,40,128]{2,1,0:T(8,128)}) fusion(f32[]{:T(128)} %bitcast.6, f32[1,2,64,40,128]{4,3,2,1,0:T(8,128)} %bitcast.480, bf16[4,2,64,40,128]{4,3,2,1,0:T(8,128)(2,1)} %param.6, f32[1,2,64,40,128]{4,3,2,1,0:T(8,128)} %bitcast.478, f32[1,2,64,40,128]{4,3,2,1,0:T(8,128)} %bitcast.479, ...), kind=kLoop, calls=%fused_computation.142 | loop fusion | flops 14417920 | bytes 22282244 | tf_op jit(solution)/shard_map/mul | solution.py:91
  590.6 39.2 %psum.15 = f32[]{:T(128)} all-reduce(f32[]{:T(128)S(6)} %add.285), channel_id=1, replica_groups=mesh['contrast'=4,'pa'=2,'pb'=4] {'contrast','pa','pb'}, use_global_device_ids=true, to_apply=%region_5.6 | all-reduce | flops 1 | bytes 8 | tf_op jit(solution)/shard_map/psum | solution.py:95
  630.5 13.9 %all-reduce.2.cloned.1.call-done = f32[64,40,128]{2,1,0:T(8,128)} async-done(((f32[64,40,128]{2,1,0:T(8,128)}), f32[64,40,128]{2,1,0:T(8,128)}) %all-reduce.2.cloned.1.call-update) | async-done | bytes 1310736 | tf_op jit(solution)/shard_map/psum | solution.py:92
  (46 shorter events, 74.6 us)
Async XLA Ops:
  19.2 6.9 %copy-start = (f32[1,2,64,40,128]{4,3,2,1,0:T(8,128)S(1)}, f32[1,2,64,40,128]{4,3,2,1,0:T(8,128)}, u32[]{:S(2)}) copy-start(f32[1,2,64,40,128]{4,3,2,1,0:T(8,128)} %param.5) | copy-start | bytes 7864324
  19.2 66.6 %all-to-all-start.6 = ((f32[1,2,128,1,2560]{4,1,3,0,2:T(2,128)}), f32[1,2,128,1,2560]{4,1,3,0,2:T(2,128)}, u32[]{:S(2)}, u32[]{:S(2)}) async-start(f32[1,2,128,1,2560]{4,1,3,0,2:T(2,128)} %copy.100), calls=%async_computation.6 | async-start | bytes 5242880 | tf_op jit(solution)/shard_map/all_to_all | solution.py:64
  85.7 63.3 %all-to-all-start.2 = ((f32[1,2,128,1,2560]{4,1,3,0,2:T(2,128)}), f32[1,2,128,1,2560]{4,1,3,0,2:T(2,128)S(1)}, u32[]{:S(2)}, u32[]{:S(2)}) async-start(f32[1,2,128,1,2560]{4,1,3,0,2:T(2,128)} %copy.80), calls=%async_computation.2 | async-start | bytes 5242880 | tf_op jit(solution)/shard_map/all_to_all | solution.py:64
  149.0 1.5 copy-start.2
  150.5 64.4 %all-to-all-start = ((f32[1,2,128,1,2560]{4,1,3,0,2:T(2,128)}), f32[1,2,128,1,2560]{4,1,3,0,2:T(2,128)}, u32[]{:S(2)}, u32[]{:S(2)}) async-start(f32[1,2,128,1,2560]{4,1,3,0,2:T(2,128)} %copy.70), calls=%async_computation | async-start | bytes 5242880 | tf_op jit(solution)/shard_map/all_to_all | solution.py:64
  214.9 75.8 %all-to-all-start.4 = ((f32[1,2,128,1,2560]{4,1,3,0,2:T(2,128)}), f32[1,2,128,1,2560]{4,1,3,0,2:T(2,128)}, u32[]{:S(2)}, u32[]{:S(2)}) async-start(f32[1,2,128,1,2560]{4,1,3,0,2:T(2,128)} %copy.90), calls=%async_computation.4 | async-start | bytes 5242880 | tf_op jit(solution)/shard_map/all_to_all | solution.py:64
  290.6 72.4 %all-to-all-start.1 = ((f32[8,2,16,1,2560]{4,2,1,3,0:T(8,128)}), f32[8,2,16,1,2560]{4,2,1,3,0:T(8,128)}, u32[]{:S(2)}, u32[]{:S(2)}) async-start(f32[8,2,16,1,2560]{4,2,1,3,0:T(8,128)} %bitcast.489), calls=%async_computation.1 | async-start | bytes 5242880 | tf_op jit(solution)/shard_map/all_to_all | solution.py:80
  363.0 72.2 %all-to-all-start.5 = ((f32[8,2,16,1,2560]{4,2,1,3,0:T(8,128)}), f32[8,2,16,1,2560]{4,2,1,3,0:T(8,128)}, u32[]{:S(2)}, u32[]{:S(2)}) async-start(f32[8,2,16,1,2560]{4,2,1,3,0:T(8,128)} %bitcast.490), calls=%async_computation.5 | async-start | bytes 5242880 | tf_op jit(solution)/shard_map/all_to_all | solution.py:80
  435.2 72.4 %all-to-all-start.3 = ((f32[8,2,16,1,2560]{4,2,1,3,0:T(8,128)}), f32[8,2,16,1,2560]{4,2,1,3,0:T(8,128)}, u32[]{:S(2)}, u32[]{:S(2)}) async-start(f32[8,2,16,1,2560]{4,2,1,3,0:T(8,128)} %bitcast.487), calls=%async_computation.3 | async-start | bytes 5242880 | tf_op jit(solution)/shard_map/all_to_all | solution.py:80
  507.5 64.8 %all-to-all-start.7 = ((f32[8,2,16,1,2560]{4,2,1,3,0:T(8,128)}), f32[8,2,16,1,2560]{4,2,1,3,0:T(8,128)S(1)}, u32[]{:S(2)}, u32[]{:S(2)}) async-start(f32[8,2,16,1,2560]{4,2,1,3,0:T(8,128)} %bitcast.488), calls=%async_computation.7 | async-start | bytes 5242880 | tf_op jit(solution)/shard_map/all_to_all | solution.py:80
  512.6 131.8 %all-reduce.2.cloned.1.call-start = ((), (), s32[]{:S(2)}) async-start(), calls=%async_computation.8 | async-start | bytes 2621440 | tf_op jit(solution)/shard_map/psum | solution.py:92
  576.4 3.5 copy-start.1
Sparse Core Ops, SparseCore 0:
  588.3 56.0 all-reduce.1
where the time goes:
time: 665 us; the launch traced here: 657 us
  waiting for transfers between devices  200 us (30%)
  matrix products  182 us (27%)
  local copies, waits for them, and re-layouts  150 us (23%)
  starting transfers between devices  40.8 us (6%)
  blocking collectives  39.2 us (6%)
  other arithmetic  26.8 us (4%)
  between operations  19.6 us (3%)
    dot_general x24, matrix products, contract(): jnp.einsum(pattern, operand, table, precision=lax.Precision.HIGHEST, pref...  182 us
    all_to_all x4, waiting for transfers between devices, per_device(): lax.all_to_all(transformed[None], ('pa', 'pb'), split_axis=2, concat_axis...  153 us
    transpose x8, local copies, waits for them, and re-layouts, contract(): jnp.einsum(pattern, operand, table, precision=lax.Precision.HIGHEST, pref...  44.9 us
    psum x1, blocking collectives, per_device(): misfit_sum = lax.psum(misfit_local, ('contrast', 'pa', 'pb'))  39.2 us
    another operation x4, local copies, waits for them, and re-layouts  35.9 us
    reshape x4, local copies, waits for them, and re-layouts, per_device(): spatial.reshape(groups_pa * groups_pb, 2, depth_share, one_members, plane...  32.4 us
    all_to_all x4, waiting for transfers between devices, per_device(): lax.all_to_all(sendable, ('pa', 'pb'), split_axis=0, concat_axis=2, tiled...  32.3 us
    all_to_all x4, starting transfers between devices, per_device(): lax.all_to_all(sendable, ('pa', 'pb'), split_axis=0, concat_axis=2, tiled...  21.3 us
  transfers between devices with their start and end apart: 9, of which 5 were waited for; matrix products, arithmetic and copies ran while one was open for 49% of the time, Pallas kernels for 0%

commit v1 on v0

v1 whole, which is shorter than its diff:
```python
import math

import jax
import jax.numpy as jnp
from jax import lax
from jax.sharding import PartitionSpec as P

step_size = 1.0
threshold = 2.5


def complex_table(length, sign_value):
    indices = lax.iota(jnp.int32, length)
    phases = indices[:, None] * indices[None, :] % length
    angles = phases.astype(jnp.float32) * (2.0 * math.pi / length)
    normalize = 1.0 / math.sqrt(length)
    real_part = jnp.cos(angles) * normalize
    imag_part = sign_value * jnp.sin(angles) * normalize
    upper_rows = jnp.stack([real_part, imag_part], axis=1)
    bottom = jnp.stack([-imag_part, real_part], axis=1)
    return jnp.stack([upper_rows, bottom], axis=0)


def contract(pattern, operand, table):
    return jnp.einsum(
        pattern, operand, table, precision=lax.Precision.HIGH, preferred_element_type=jnp.float32
    )


def per_device(image, coil_maps, kspace, sampling, available):
    groups_pa = lax.axis_size("pa")
    groups_pb = lax.axis_size("pb")
    pixels = image[0]
    x_rows = pixels.shape[1]
    y_rows = pixels.shape[2]
    depth_size = pixels.shape[3]
    width_x = x_rows * groups_pa
    width_y = y_rows * groups_pb
    plane_size = x_rows * y_rows
    coil_total = coil_maps.shape[0]
    depth_share = kspace.shape[3]
    present = available[0].astype(jnp.float32)
    weight_factor = sampling[0].astype(jnp.float32) * present
    forward_z = complex_table(depth_size, -1.0)
    forward_y = complex_table(width_y, -1.0).reshape(2, groups_pb, y_rows, 2, width_y)
    forward_x = complex_table(width_x, -1.0).reshape(2, groups_pa, x_rows, 2, width_x)
    inverse_z = complex_table(depth_size, 1.0)
    inverse_y = complex_table(width_y, 1.0).reshape(2, width_y, 2, groups_pb, y_rows)
    inverse_x = complex_table(width_x, 1.0).reshape(2, width_x, 2, groups_pa, x_rows)
    every_axis = ("contrast", "pa", "pb")
    members_total = lax.axis_size("contrast") * groups_pa * groups_pb

    def sensitivity(coil_index):
        return (
            coil_maps[coil_index, 0].astype(jnp.float32),
            coil_maps[coil_index, 1].astype(jnp.float32),
        )

    def prepare(coil_index):
        sens_re, sens_im = sensitivity(coil_index)
        prod_re = sens_re * pixels[0] - sens_im * pixels[1]
        prod_im = sens_re * pixels[1] + sens_im * pixels[0]
        spread = jnp.stack([prod_re, prod_im], axis=0).reshape(2, plane_size, depth_size)
        return contract("cmz,czdk->dkm", spread, forward_z)[None]

    def exchange_forward(transformed):
        return lax.all_to_all(transformed, ("pa", "pb"), split_axis=2, concat_axis=0, tiled=True)

    def exchange_back(sendable):
        return lax.all_to_all(sendable, ("pa", "pb"), split_axis=0, concat_axis=2, tiled=True)[0]

    def fourier(portion, coil_index):
        blocks = portion.reshape(groups_pa, groups_pb, 2, depth_share, x_rows, y_rows)
        partial_value = contract("aeczxy,ceyfl->afzxl", blocks, forward_y)
        fourier_coefficients = contract("afzxl,faxdk->dzlk", partial_value, forward_x)
        kspace_residual = weight_factor * (
            fourier_coefficients - kspace[0, coil_index].astype(jnp.float32)
        )
        misfit_part = jnp.sum(kspace_residual * kspace_residual)
        one_partial_value = contract("czlk,ckfax->afzlx", kspace_residual, inverse_x)
        spatial = contract("afzlx,fldey->aedzxy", one_partial_value, inverse_y)
        return (
            spatial.reshape(groups_pa * groups_pb, 2, depth_share, plane_size),
            misfit_part,
        )

    def recover(received, coil_index, first_row, rows):
        image_part = contract("ckm,ckdz->dmz", received, inverse_z)
        image_part = image_part.reshape(2, rows, y_rows, depth_size)
        sens_re, sens_im = sensitivity(coil_index)
        sens_re = sens_re[first_row : first_row + rows]
        sens_im = sens_im[first_row : first_row + rows]
        return (
            sens_re * image_part[0] + sens_im * image_part[1],
            sens_re * image_part[1] - sens_im * image_part[0],
        )

    cut = x_rows - x_rows // 4
    halves = ((0, cut), (cut, x_rows - cut))
    last = coil_total - 1
    arrivals = {}
    outgoing = {}
    returned = {}
    misfit_parts = {}
    sent = [prepare(coil_index) for coil_index in range(coil_total)]
    steps = exchange_order(coil_total)
    for kind, coil_index in steps:
        if kind == "forward":
            arrivals[coil_index] = exchange_forward(sent[coil_index])
        else:
            returned[coil_index] = exchange_back(outgoing[coil_index])
        if kind == "forward":
            outgoing[coil_index], misfit_parts[coil_index] = fourier(
                arrivals[coil_index], coil_index
            )
    misfit_local = sum(misfit_parts[coil_index] for coil_index in range(coil_total))
    scalar_block = jnp.full((members_total, 128), misfit_local, jnp.float32)
    gathered = lax.all_to_all(
        scalar_block, every_axis, split_axis=0, concat_axis=0, tiled=True
    )
    misfit_sum = jnp.sum(gathered[:, 0])
    final = []
    for first_row, rows in halves:
        piece = outgoing[last][..., first_row * y_rows : (first_row + rows) * y_rows]
        final.append(exchange_back(piece))
    total_re = pixels[0]
    total_im = pixels[1]
    for coil_index in range(last):
        one_re, one_im = recover(returned[coil_index], coil_index, 0, x_rows)
        total_re = total_re - step_size * one_re
        total_im = total_im - step_size * one_im
    total_re, total_im = lax.optimization_barrier((total_re, total_im))
    results = []
    for (first_row, rows), piece in zip(halves, final):
        one_re, one_im = recover(piece, last, first_row, rows)
        moved_re = total_re[first_row : first_row + rows] - step_size * one_re
        moved_im = total_im[first_row : first_row + rows] - step_size * one_im
        energy = present * (moved_re * moved_re + moved_im * moved_im)
        moved_re, moved_im, energy = lax.optimization_barrier((moved_re, moved_im, energy))
        energy_total = sum_contrasts(energy)
        norm_value = jnp.sqrt(energy_total)
        factor = jnp.maximum(norm_value - threshold, 0.0) / jnp.maximum(norm_value, threshold)
        shrink = present * factor
        results.append(jnp.stack([moved_re * shrink, moved_im * shrink], axis=0))
    result = jnp.concatenate(results, axis=1)[None]
    count_all = (
        lax.axis_size("contrast") * image.shape[0] * coil_total * width_x * width_y * depth_size
    )
    return (result, misfit_sum / (2.0 * count_all))


def exchange_order(coil_total):
    steps = [("forward", coil_index) for coil_index in range(min(2, coil_total))]
    for coil_index in range(coil_total):
        if coil_index + 2 < coil_total:
            steps.append(("forward", coil_index + 2))
        if coil_index < coil_total - 1:
            steps.append(("back", coil_index))
    return steps


def sum_contrasts(energy):
    size = lax.axis_size("contrast")
    if size & (size - 1):
        return lax.psum(energy, "contrast")
    strides = [1 << bit for bit in range(size.bit_length() - 1)]
    middle = energy.shape[0] // 2
    pieces = []
    for part, order in ((energy[:middle], strides), (energy[middle:], strides[::-1])):
        for stride in order:
            pairs = [(index, index ^ stride) for index in range(size)]
            part = part + lax.ppermute(part, "contrast", pairs)
        pieces.append(part)
    return jnp.concatenate(pieces, axis=0)


def solution(mesh):
    return jax.shard_map(
        per_device,
        mesh=mesh,
        in_specs=(
            P("contrast", None, "pa", "pb", None),
            P(None, None, "pa", "pb", None),
            P("contrast", None, None, ("pa", "pb"), None, None),
            P("contrast", ("pa", "pb"), None, None),
            P("contrast"),
        ),
        out_specs=(P("contrast", None, "pa", "pb", None), P()),
        check_vma=False,
    )
```

time: 665 us -> 619 us (0.931)
  matrix products: 182 us -> 109 us
  blocking collectives: 39.2 us -> 9.27 us
  waiting for transfers between devices: 200 us -> 229 us
  local copies, waits for them, and re-layouts: 150 us -> 172 us
  between operations: 19.6 us -> 6.9 us
  starting transfers between devices: 40.8 us -> 49.5 us
    dot_general x24 -> x25, matrix products: 182 us -> 109 us  [contract(): jnp.einsum(pattern, operand, table, precision=lax.Precision.HIGH, preferr...]
    psum x1 -> x0, blocking collectives: 39.2 us -> none  [per_device(): misfit_sum = lax.psum(misfit_local, ('contrast', 'pa', 'pb'))]
    another operation x4 -> x0, local copies, waits for them, and re-layouts: 35.9 us -> none
    reshape x4 -> x8, local copies, waits for them, and re-layouts: 32.4 us -> 68.3 us  [the longest x4 35.9 us: fourier(): portion.reshape(groups_pa, groups_pb, 2, depth_share, x_rows, y_rows)]
    all_to_all x8 -> x9, waiting for transfers between devices: 186 us -> 217 us  [the longest x4 159 us: exchange_forward(): lax.all_to_all(transformed, ('pa', 'pb'), split_axis=2, concat_axis=0, ti...]
    slice x0 -> x19, local copies, waits for them, and re-layouts: none -> 30.4 us  [the longest x10 15.8 us: recover(): image_part[1]]
    psum x1 -> x0, waiting for transfers between devices: 13.9 us -> none  [per_device(): energy_total = lax.psum(energy, 'contrast')]
    transpose x8 -> x4, local copies, waits for them, and re-layouts: 44.9 us -> 31.7 us  [contract(): jnp.einsum(pattern, operand, table, precision=lax.Precision.HIGH, preferr...]
  transfers between devices with their start and end apart: 9 -> 17, of which waited for: 5 -> 11; matrix products, arithmetic and copies ran while one was open for 49% -> 45% of each run, Pallas kernels for 0% -> 0%
where the time goes in v1:
time: 619 us; the launch traced here: 609 us
  waiting for transfers between devices  229 us (37%)
  local copies, waits for them, and re-layouts  172 us (28%)
  matrix products  109 us (18%)
  starting transfers between devices  49.5 us (8%)
  other arithmetic  32.4 us (5%)
  blocking collectives  9.27 us (1%)
  between operations  6.9 us (1%)
    all_to_all x4, waiting for transfers between devices, exchange_forward(): lax.all_to_all(transformed, ('pa', 'pb'), split_axis=2, concat_axis=0, ti...  159 us
    dot_general x25, matrix products, contract(): jnp.einsum(pattern, operand, table, precision=lax.Precision.HIGH, preferr...  109 us
    all_to_all x5, waiting for transfers between devices, exchange_back(): lax.all_to_all(sendable, ('pa', 'pb'), split_axis=0, concat_axis=2, tiled...  58.5 us
    reshape x4, local copies, waits for them, and re-layouts, fourier(): portion.reshape(groups_pa, groups_pb, 2, depth_share, x_rows, y_rows)  35.9 us
    reshape x4, local copies, waits for them, and re-layouts, fourier(): spatial.reshape(groups_pa * groups_pb, 2, depth_share, plane_size)  32.4 us
    transpose x4, local copies, waits for them, and re-layouts, contract(): jnp.einsum(pattern, operand, table, precision=lax.Precision.HIGH, preferr...  31.7 us
    all_to_all x5, starting transfers between devices, exchange_back(): lax.all_to_all(sendable, ('pa', 'pb'), split_axis=0, concat_axis=2, tiled...  21.6 us
    all_to_all x4, starting transfers between devices, exchange_forward(): lax.all_to_all(transformed, ('pa', 'pb'), split_axis=2, concat_axis=0, ti...  19.5 us
  transfers between devices with their start and end apart: 17, of which 11 were waited for; matrix products, arithmetic and copies ran while one was open for 45% of the time, Pallas kernels for 0%

profile of v1, /device:TPU:0, one launch (start us, length us, event | category | flops | bytes accessed | tf_op | source)
XLA Modules:
  0.0 608.5 jit_solution(15992090021329937605)
XLA Ops:
  1.4 4.7 fusion.92
  11.1 6.6 %all-to-all-start.4 = ((f32[1,2,128,2560]{3,1,0,2:T(2,128)}), f32[1,2,128,2560]{3,1,0,2:T(2,128)}, u32[]{:S(2)}, u32[]{:S(2)}) async-start(f32[1,2,128,2560]{3,1,0,2:T(2,128)} %copy.151), calls=%async_computation.4 | async-start | bytes 5242880 | tf_op jit(solution)/shard_map/all_to_all | solution.py:67
  17.7 3.9 fusion.88
  26.5 51.0 %all-to-all-done.4 = f32[1,2,128,2560]{3,1,0,2:T(2,128)} async-done(((f32[1,2,128,2560]{3,1,0,2:T(2,128)}), f32[1,2,128,2560]{3,1,0,2:T(2,128)}, u32[]{:S(2)}, u32[]{:S(2)}) %all-to-all-start.4) | async-done | bytes 2621472 | tf_op jit(solution)/shard_map/all_to_all | solution.py:67
  77.5 3.8 all-to-all-start
  87.9 53.1 %all-to-all-done = f32[1,2,128,2560]{3,1,0,2:T(2,128)S(1)} async-done(((f32[1,2,128,2560]{3,1,0,2:T(2,128)}), f32[1,2,128,2560]{3,1,0,2:T(2,128)S(1)}, u32[]{:S(2)}, u32[]{:S(2)}) %all-to-all-start) | async-done | bytes 2621472 | tf_op jit(solution)/shard_map/all_to_all | solution.py:67
  142.5 4.4 all-to-all-start.6
  153.4 53.2 %all-to-all-done.6 = f32[1,2,128,2560]{3,1,0,2:T(2,128)} async-done(((f32[1,2,128,2560]{3,1,0,2:T(2,128)}), f32[1,2,128,2560]{3,1,0,2:T(2,128)}, u32[]{:S(2)}, u32[]{:S(2)}) %all-to-all-start.6) | async-done | bytes 2621472 | tf_op jit(solution)/shard_map/all_to_all | solution.py:67
  206.6 4.7 all-to-all-start.2
  215.9 3.7 copy.248
  219.6 9.0 %reshape.828 = f32[2,4,2,16,64,40]{5,4,3,2,1,0:T(8,128)} reshape(f32[8,1,2,16,2560]{4,3,2,0,1:T(8,128)} %bitcast.535) | data formatting | bytes 5242880 | tf_op jit(solution)/shard_map/reshape | solution.py:73
  228.6 9.3 %fusion = f32[2,160,2,16,64,1,1]{1,4,6,5,0,2,3:T(8,128)S(1)} fusion(f32[1,4,40,1,160]{4,2,1,0,3:T(8,128)S(1)} %get-tuple-element.65, f32[1,4,40,1,160]{4,2,1,0,3:T(8,128)S(1)} %get-tuple-element.64, f32[1,4,40,1,160]{4,2,1,0,3:T(8,128)S(1)} %get-tuple-element.63, f32[2,4,2,16,64,40]{5,4,3,2,1,0:T(8,128)} %reshape.828), kind=kOutput, calls=%fused_computation | convolution fusion | flops 1258598400 | bytes 5550080 | tf_op jit(solution)/shard_map/aeczxy,ceyfl->afzxl/dot_general | solution.py:25
  238.0 5.5 multiply_reduce_fusion
  245.5 6.1 fusion.53
  251.6 7.9 %copy.163 = f32[2,4,2,16,64,40]{5,4,3,2,1,0:T(8,128)} copy(f32[2,4,2,16,64,40]{4,5,3,0,1,2:T(8,128)} %fusion.53) | data formatting | bytes 5242880 | tf_op jit(solution)/shard_map/afzlx,fldey->aedzxy/transpose | solution.py:25
  259.5 8.1 %reshape.829 = f32[8,2,16,2560]{3,2,1,0:T(8,128)} reshape(f32[2,4,2,16,64,40]{5,4,3,2,1,0:T(8,128)} %copy.163) | data formatting | bytes 5242880 | tf_op jit(solution)/shard_map/reshape | solution.py:83
  277.6 14.6 %all-to-all-done.8 = f32[8,2,16,640]{3,2,1,0:T(8,128)S(1)} async-done(((f32[8,2,16,640]{3,2,1,0:T(8,128)}), f32[8,2,16,640]{3,2,1,0:T(8,128)S(1)}, u32[]{:S(2)}, u32[]{:S(2)}) %all-to-all-start.8) | async-done | bytes 655392 | tf_op jit(solution)/shard_map/all_to_all | solution.py:70
  293.1 3.8 all-to-all-start.7
  296.9 3.7 copy.249
  300.6 9.0 %reshape.826 = f32[2,4,2,16,64,40]{5,4,3,2,1,0:T(8,128)} reshape(f32[8,1,2,16,2560]{4,3,2,0,1:T(8,128)} %bitcast.536) | data formatting | bytes 5242880 | tf_op jit(solution)/shard_map/reshape | solution.py:73
  309.5 10.1 %fusion.2 = f32[2,160,2,16,64,1,1]{1,4,6,5,0,2,3:T(8,128)S(1)} fusion(f32[1,4,40,1,160]{4,2,1,0,3:T(8,128)} %copy-done.54, f32[1,4,40,1,160]{4,2,1,0,3:T(8,128)} %copy-done.53, f32[1,4,40,1,160]{4,2,1,0,3:T(8,128)} %copy-done.52, f32[2,4,2,16,64,40]{5,4,3,2,1,0:T(8,128)} %reshape.826), kind=kOutput, calls=%fused_computation.2 | convolution fusion | flops 1258598400 | bytes 5550080 | tf_op jit(solution)/shard_map/aeczxy,ceyfl->afzxl/dot_general | solution.py:25
  319.7 5.6 multiply_reduce_fusion.1
  327.3 6.1 fusion.50
  333.4 7.9 %copy.155 = f32[2,4,2,16,64,40]{5,4,3,2,1,0:T(8,128)} copy(f32[2,4,2,16,64,40]{4,5,3,0,1,2:T(8,128)} %fusion.50) | data formatting | bytes 5242880 | tf_op jit(solution)/shard_map/afzlx,fldey->aedzxy/transpose | solution.py:25
  341.3 8.1 %reshape.827 = f32[8,2,16,2560]{3,2,1,0:T(8,128)} reshape(f32[2,4,2,16,64,40]{5,4,3,2,1,0:T(8,128)} %copy.155) | data formatting | bytes 5242880 | tf_op jit(solution)/shard_map/reshape | solution.py:83
  349.4 5.5 all-to-all-start.5
  354.9 3.7 copy.251
  358.6 9.0 %reshape.822 = f32[2,4,2,16,64,40]{5,4,3,2,1,0:T(8,128)} reshape(f32[8,1,2,16,2560]{4,3,2,0,1:T(8,128)} %bitcast.537) | data formatting | bytes 5242880 | tf_op jit(solution)/shard_map/reshape | solution.py:73
  367.5 10.1 %fusion.6 = f32[2,160,2,16,64,1,1]{1,4,6,5,0,2,3:T(8,128)S(1)} fusion(f32[1,4,40,1,160]{4,2,1,0,3:T(8,128)} %copy-done.54, f32[1,4,40,1,160]{4,2,1,0,3:T(8,128)} %copy-done.53, f32[1,4,40,1,160]{4,2,1,0,3:T(8,128)} %copy-done.52, f32[2,4,2,16,64,40]{5,4,3,2,1,0:T(8,128)} %reshape.822), kind=kOutput, calls=%fused_computation.6 | convolution fusion | flops 1258598400 | bytes 5550080 | tf_op jit(solution)/shard_map/aeczxy,ceyfl->afzxl/dot_general | solution.py:25
  377.7 5.6 multiply_reduce_fusion.3
  385.3 6.2 %fusion.44 = f32[2,4,2,16,64,40]{4,5,3,0,1,2:T(8,128)} fusion(f32[2,2,64,16,160,1]{4,2,5,0,3,1:T(8,128)S(1)} %fusion.42, f32[1,160,1,4,40]{1,4,0,3,2:T(8,128)S(1)} %copy-done.20, f32[1,160,1,4,40]{1,4,0,3,2:T(8,128)S(1)} %copy-done.16, f32[1,160,1,4,40]{1,4,0,3,2:T(8,128)S(1)} %copy-done.12), kind=kOutput, calls=%fused_computation.69 | convolution fusion | flops 1258598400 | bytes 5550080 | tf_op jit(solution)/shard_map/afzlx,fldey->aedzxy/dot_general | solution.py:25
  391.5 7.9 %copy.139 = f32[2,4,2,16,64,40]{5,4,3,2,1,0:T(8,128)} copy(f32[2,4,2,16,64,40]{4,5,3,0,1,2:T(8,128)} %fusion.44) | data formatting | bytes 5242880 | tf_op jit(solution)/shard_map/afzlx,fldey->aedzxy/transpose | solution.py:25
  399.5 8.1 %reshape.823 = f32[8,2,16,2560]{3,2,1,0:T(8,128)} reshape(f32[2,4,2,16,64,40]{5,4,3,2,1,0:T(8,128)} %copy.139) | data formatting | bytes 5242880 | tf_op jit(solution)/shard_map/reshape | solution.py:83
  407.6 7.0 %all-to-all-done.5 = f32[8,2,16,2560]{3,2,1,0:T(8,128)} async-done(((f32[8,2,16,2560]{3,2,1,0:T(8,128)}), f32[8,2,16,2560]{3,2,1,0:T(8,128)}, u32[]{:S(2)}, u32[]{:S(2)}) %all-to-all-start.5) | async-done | bytes 2621472 | tf_op jit(solution)/shard_map/all_to_all | solution.py:70
  414.6 4.4 all-to-all-start.1
  419.0 3.7 copy.250
  422.7 9.0 %reshape.824 = f32[2,4,2,16,64,40]{5,4,3,2,1,0:T(8,128)} reshape(f32[8,1,2,16,2560]{4,3,2,0,1:T(8,128)} %bitcast.538) | data formatting | bytes 5242880 | tf_op jit(solution)/shard_map/reshape | solution.py:73
  431.7 10.1 %fusion.4 = f32[2,160,2,16,64,1,1]{1,4,6,5,0,2,3:T(8,128)S(1)} fusion(f32[1,4,40,1,160]{4,2,1,0,3:T(8,128)} %copy-done.54, f32[1,4,40,1,160]{4,2,1,0,3:T(8,128)} %copy-done.53, f32[1,4,40,1,160]{4,2,1,0,3:T(8,128)} %copy-done.52, f32[2,4,2,16,64,40]{5,4,3,2,1,0:T(8,128)} %reshape.824), kind=kOutput, calls=%fused_computation.4 | convolution fusion | flops 1258598400 | bytes 5550080 | tf_op jit(solution)/shard_map/aeczxy,ceyfl->afzxl/dot_general | solution.py:25
  441.8 5.6 multiply_reduce_fusion.2
  449.5 6.3 %fusion.47 = f32[2,4,2,16,64,40]{4,5,3,0,1,2:T(8,128)} fusion(f32[2,2,64,16,160,1]{4,2,5,0,3,1:T(8,128)S(1)} %fusion.40, f32[1,160,1,4,40]{1,4,0,3,2:T(8,128)S(1)} %copy-done.21, f32[1,160,1,4,40]{1,4,0,3,2:T(8,128)S(1)} %copy-done.17, f32[1,160,1,4,40]{1,4,0,3,2:T(8,128)S(1)} %copy-done.13), kind=kOutput, calls=%fused_computation.70 | convolution fusion | flops 1258598400 | bytes 5550080 | tf_op jit(solution)/shard_map/afzlx,fldey->aedzxy/dot_general | solution.py:25
  455.7 7.9 %copy.147 = f32[2,4,2,16,64,40]{5,4,3,2,1,0:T(8,128)} copy(f32[2,4,2,16,64,40]{4,5,3,0,1,2:T(8,128)} %fusion.47) | data formatting | bytes 5242880 | tf_op jit(solution)/shard_map/afzlx,fldey->aedzxy/transpose | solution.py:25
  463.7 8.1 %reshape.825 = f32[8,2,16,2560]{3,2,1,0:T(8,128)} reshape(f32[2,4,2,16,64,40]{5,4,3,2,1,0:T(8,128)} %copy.147) | data formatting | bytes 5242880 | tf_op jit(solution)/shard_map/reshape | solution.py:83
  471.8 7.0 %all-to-all-done.1 = f32[8,2,16,2560]{3,2,1,0:T(8,128)} async-done(((f32[8,2,16,2560]{3,2,1,0:T(8,128)}), f32[8,2,16,2560]{3,2,1,0:T(8,128)}, u32[]{:S(2)}, u32[]{:S(2)}) %all-to-all-start.1) | async-done | bytes 2621472 | tf_op jit(solution)/shard_map/all_to_all | solution.py:70
  478.7 4.4 all-to-all-start.3
  513.0 29.9 %all-to-all-done.3 = f32[8,2,16,2560]{3,2,1,0:T(8,128)} async-done(((f32[8,2,16,2560]{3,2,1,0:T(8,128)}), f32[8,2,16,2560]{3,2,1,0:T(8,128)}, u32[]{:S(2)}, u32[]{:S(2)}) %all-to-all-start.3) | async-done | bytes 2621472 | tf_op jit(solution)/shard_map/all_to_all | solution.py:70
  553.5 5.3 fusion.79
  569.6 9.1 %collective-permute-done = f32[24,40,128]{2,1,0:T(8,128)S(1)} collective-permute-done((f32[24,40,128]{2,1,0:T(8,128)S(1)}, f32[24,40,128]{2,1,0:T(8,128)S(1)}, u32[]{:S(2)}, u32[]{:S(2)}) %collective-permute-start) | collective-permute-done | bytes 491552 | tf_op jit(solution)/shard_map/ppermute | solution.py:172
  589.0 9.3 %all_to_all.144 = f32[32,1,128]{2,1,0:T(1,128)S(1)} all-to-all(f32[32,1,128]{2,1,0:T(1,128)S(1)} %broadcast_in_dim.17), channel_id=1, replica_groups=mesh['contrast'=4,'pa'=2,'pb'=4] {'contrast','pa','pb'}, dimensions={0} | all-to-all | bytes 32768 | tf_op jit(solution)/shard_map/all_to_all | solution.py:118
  (200 shorter events, 114.8 us)
Async XLA Ops:
  11.1 6.6 %copy-start = (f32[1,2,64,40,128]{4,3,2,1,0:T(8,128)S(1)}, f32[1,2,64,40,128]{4,3,2,1,0:T(8,128)}, u32[]{:S(2)}) copy-start(f32[1,2,64,40,128]{4,3,2,1,0:T(8,128)} %param.5) | copy-start | bytes 7864324
  11.1 66.4 %all-to-all-start.4 = ((f32[1,2,128,2560]{3,1,0,2:T(2,128)}), f32[1,2,128,2560]{3,1,0,2:T(2,128)}, u32[]{:S(2)}, u32[]{:S(2)}) async-start(f32[1,2,128,2560]{3,1,0,2:T(2,128)} %copy.151), calls=%async_computation.4 | async-start | bytes 5242880 | tf_op jit(solution)/shard_map/all_to_all | solution.py:67
  77.5 63.5 %all-to-all-start = ((f32[1,2,128,2560]{3,1,0,2:T(2,128)}), f32[1,2,128,2560]{3,1,0,2:T(2,128)S(1)}, u32[]{:S(2)}, u32[]{:S(2)}) async-start(f32[1,2,128,2560]{3,1,0,2:T(2,128)} %copy.135), calls=%async_computation | async-start | bytes 5242880 | tf_op jit(solution)/shard_map/all_to_all | solution.py:67
  142.5 64.1 %all-to-all-start.6 = ((f32[1,2,128,2560]{3,1,0,2:T(2,128)}), f32[1,2,128,2560]{3,1,0,2:T(2,128)}, u32[]{:S(2)}, u32[]{:S(2)}) async-start(f32[1,2,128,2560]{3,1,0,2:T(2,128)} %copy.159), calls=%async_computation.6 | async-start | bytes 5242880 | tf_op jit(solution)/shard_map/all_to_all | solution.py:67
  206.6 64.4 %all-to-all-start.2 = ((f32[1,2,128,2560]{3,1,0,2:T(2,128)}), f32[1,2,128,2560]{3,1,0,2:T(2,128)}, u32[]{:S(2)}, u32[]{:S(2)}) async-start(f32[1,2,128,2560]{3,1,0,2:T(2,128)} %copy.143), calls=%async_computation.2 | async-start | bytes 5242880 | tf_op jit(solution)/shard_map/all_to_all | solution.py:67
  212.3 25.6 %copy-start.38 = (f32[1,2,64,1,128]{4,2,0,1,3:T(8,128)}, f32[1,2,64,1,128]{4,2,0,1,3:T(8,128)S(1)}, u32[]{:S(2)}) copy-start(f32[1,2,64,1,128]{4,2,0,1,3:T(8,128)S(1)} %get-tuple-element.69) | copy-start | bytes 196612
  212.3 25.6 %copy-start.42 = (f32[1,2,64,1,128]{4,2,0,1,3:T(8,128)}, f32[1,2,64,1,128]{4,2,0,1,3:T(8,128)S(1)}, u32[]{:S(2)}) copy-start(f32[1,2,64,1,128]{4,2,0,1,3:T(8,128)S(1)} %get-tuple-element.70) | copy-start | bytes 196612
  212.3 25.6 %copy-start.46 = (f32[1,2,64,1,128]{4,2,0,1,3:T(8,128)}, f32[1,2,64,1,128]{4,2,0,1,3:T(8,128)S(1)}, u32[]{:S(2)}) copy-start(f32[1,2,64,1,128]{4,2,0,1,3:T(8,128)S(1)} %get-tuple-element.71) | copy-start | bytes 196612
  212.7 30.8 %copy-start.26 = (f32[1,128,1,2,64]{1,4,0,2,3:T(8,128)}, f32[1,128,1,2,64]{1,4,0,2,3:T(8,128)S(1)}, u32[]{:S(2)}) copy-start(f32[1,128,1,2,64]{1,4,0,2,3:T(8,128)S(1)} %get-tuple-element.66) | copy-start | bytes 196612
  212.7 30.8 %copy-start.30 = (f32[1,128,1,2,64]{1,4,0,2,3:T(8,128)}, f32[1,128,1,2,64]{1,4,0,2,3:T(8,128)S(1)}, u32[]{:S(2)}) copy-start(f32[1,128,1,2,64]{1,4,0,2,3:T(8,128)S(1)} %get-tuple-element.67) | copy-start | bytes 196612
  212.7 30.8 %copy-start.34 = (f32[1,128,1,2,64]{1,4,0,2,3:T(8,128)}, f32[1,128,1,2,64]{1,4,0,2,3:T(8,128)S(1)}, u32[]{:S(2)}) copy-start(f32[1,128,1,2,64]{1,4,0,2,3:T(8,128)S(1)} %get-tuple-element.68) | copy-start | bytes 196612
  213.5 15.1 %copy-start.52 = (f32[1,4,40,1,160]{4,2,1,0,3:T(8,128)}, f32[1,4,40,1,160]{4,2,1,0,3:T(8,128)S(1)}, u32[]{:S(2)}) copy-start(f32[1,4,40,1,160]{4,2,1,0,3:T(8,128)S(1)} %get-tuple-element.63) | copy-start | bytes 307204
  213.5 15.1 %copy-start.53 = (f32[1,4,40,1,160]{4,2,1,0,3:T(8,128)}, f32[1,4,40,1,160]{4,2,1,0,3:T(8,128)S(1)}, u32[]{:S(2)}) copy-start(f32[1,4,40,1,160]{4,2,1,0,3:T(8,128)S(1)} %get-tuple-element.64) | copy-start | bytes 307204
  213.5 15.1 %copy-start.54 = (f32[1,4,40,1,160]{4,2,1,0,3:T(8,128)}, f32[1,4,40,1,160]{4,2,1,0,3:T(8,128)S(1)}, u32[]{:S(2)}) copy-start(f32[1,4,40,1,160]{4,2,1,0,3:T(8,128)S(1)} %get-tuple-element.65) | copy-start | bytes 307204
  214.3 31.2 %copy-start.10 = (f32[1,160,1,4,40]{1,4,0,3,2:T(8,128)}, f32[1,160,1,4,40]{1,4,0,3,2:T(8,128)S(1)}, u32[]{:S(2)}) copy-start(f32[1,160,1,4,40]{1,4,0,3,2:T(8,128)S(1)} %get-tuple-element.60) | copy-start | bytes 307204
  214.3 31.2 %copy-start.14 = (f32[1,160,1,4,40]{1,4,0,3,2:T(8,128)}, f32[1,160,1,4,40]{1,4,0,3,2:T(8,128)S(1)}, u32[]{:S(2)}) copy-start(f32[1,160,1,4,40]{1,4,0,3,2:T(8,128)S(1)} %get-tuple-element.61) | copy-start | bytes 307204
  214.3 31.2 %copy-start.18 = (f32[1,160,1,4,40]{1,4,0,3,2:T(8,128)}, f32[1,160,1,4,40]{1,4,0,3,2:T(8,128)S(1)}, u32[]{:S(2)}) copy-start(f32[1,160,1,4,40]{1,4,0,3,2:T(8,128)S(1)} %get-tuple-element.62) | copy-start | bytes 307204
  271.0 21.2 %all-to-all-start.8 = ((f32[8,2,16,640]{3,2,1,0:T(8,128)}), f32[8,2,16,640]{3,2,1,0:T(8,128)S(1)}, u32[]{:S(2)}, u32[]{:S(2)}) async-start(f32[8,2,16,640]{3,2,1,0:T(8,128)} %slice.232), calls=%async_computation.8 | async-start | bytes 1310720 | tf_op jit(solution)/shard_map/all_to_all | solution.py:70
  293.1 56.3 %all-to-all-start.7 = ((f32[8,2,16,1920]{3,2,1,0:T(8,128)}), f32[8,2,16,1920]{3,2,1,0:T(8,128)S(1)}, u32[]{:S(2)}, u32[]{:S(2)}) async-start(f32[8,2,16,1920]{3,2,1,0:T(8,128)} %slice.227), calls=%async_computation.7 | async-start | bytes 3932160 | tf_op jit(solution)/shard_map/all_to_all | solution.py:70
  309.5 10.1 %copy-start.39 = (f32[1,2,64,1,128]{4,2,0,1,3:T(8,128)S(1)}, f32[1,2,64,1,128]{4,2,0,1,3:T(8,128)}, u32[]{:S(2)}) copy-start(f32[1,2,64,1,128]{4,2,0,1,3:T(8,128)} %copy-done.38) | copy-start | bytes 196612
  309.5 10.1 %copy-start.43 = (f32[1,2,64,1,128]{4,2,0,1,3:T(8,128)S(1)}, f32[1,2,64,1,128]{4,2,0,1,3:T(8,128)}, u32[]{:S(2)}) copy-start(f32[1,2,64,1,128]{4,2,0,1,3:T(8,128)} %copy-done.42) | copy-start | bytes 196612
  309.5 10.1 %copy-start.47 = (f32[1,2,64,1,128]{4,2,0,1,3:T(8,128)S(1)}, f32[1,2,64,1,128]{4,2,0,1,3:T(8,128)}, u32[]{:S(2)}) copy-start(f32[1,2,64,1,128]{4,2,0,1,3:T(8,128)} %copy-done.46) | copy-start | bytes 196612
  349.4 65.2 %all-to-all-start.5 = ((f32[8,2,16,2560]{3,2,1,0:T(8,128)}), f32[8,2,16,2560]{3,2,1,0:T(8,128)}, u32[]{:S(2)}, u32[]{:S(2)}) async-start(f32[8,2,16,2560]{3,2,1,0:T(8,128)} %reshape.827), calls=%async_computation.5 | async-start | bytes 5242880 | tf_op jit(solution)/shard_map/all_to_all | solution.py:70
  367.5 10.1 %copy-start.40 = (f32[1,2,64,1,128]{4,2,0,1,3:T(8,128)S(1)}, f32[1,2,64,1,128]{4,2,0,1,3:T(8,128)}, u32[]{:S(2)}) copy-start(f32[1,2,64,1,128]{4,2,0,1,3:T(8,128)} %copy-done.38) | copy-start | bytes 196612
  367.5 10.1 %copy-start.44 = (f32[1,2,64,1,128]{4,2,0,1,3:T(8,128)S(1)}, f32[1,2,64,1,128]{4,2,0,1,3:T(8,128)}, u32[]{:S(2)}) copy-start(f32[1,2,64,1,128]{4,2,0,1,3:T(8,128)} %copy-done.42) | copy-start | bytes 196612
  367.5 10.1 %copy-start.48 = (f32[1,2,64,1,128]{4,2,0,1,3:T(8,128)S(1)}, f32[1,2,64,1,128]{4,2,0,1,3:T(8,128)}, u32[]{:S(2)}) copy-start(f32[1,2,64,1,128]{4,2,0,1,3:T(8,128)} %copy-done.46) | copy-start | bytes 196612
  414.6 64.1 %all-to-all-start.1 = ((f32[8,2,16,2560]{3,2,1,0:T(8,128)}), f32[8,2,16,2560]{3,2,1,0:T(8,128)}, u32[]{:S(2)}, u32[]{:S(2)}) async-start(f32[8,2,16,2560]{3,2,1,0:T(8,128)} %reshape.823), calls=%async_computation.1 | async-start | bytes 5242880 | tf_op jit(solution)/shard_map/all_to_all | solution.py:70
  431.7 10.1 %copy-start.41 = (f32[1,2,64,1,128]{4,2,0,1,3:T(8,128)S(1)}, f32[1,2,64,1,128]{4,2,0,1,3:T(8,128)}, u32[]{:S(2)}) copy-start(f32[1,2,64,1,128]{4,2,0,1,3:T(8,128)} %copy-done.38) | copy-start | bytes 196612
  431.7 10.1 %copy-start.45 = (f32[1,2,64,1,128]{4,2,0,1,3:T(8,128)S(1)}, f32[1,2,64,1,128]{4,2,0,1,3:T(8,128)}, u32[]{:S(2)}) copy-start(f32[1,2,64,1,128]{4,2,0,1,3:T(8,128)} %copy-done.42) | copy-start | bytes 196612
  431.7 10.1 %copy-start.49 = (f32[1,2,64,1,128]{4,2,0,1,3:T(8,128)S(1)}, f32[1,2,64,1,128]{4,2,0,1,3:T(8,128)}, u32[]{:S(2)}) copy-start(f32[1,2,64,1,128]{4,2,0,1,3:T(8,128)} %copy-done.46) | copy-start | bytes 196612
  441.8 5.7 copy-start.29
  441.8 5.6 copy-start.33
  478.7 64.1 %all-to-all-start.3 = ((f32[8,2,16,2560]{3,2,1,0:T(8,128)}), f32[8,2,16,2560]{3,2,1,0:T(8,128)}, u32[]{:S(2)}, u32[]{:S(2)}) async-start(f32[8,2,16,2560]{3,2,1,0:T(8,128)} %reshape.825), calls=%async_computation.3 | async-start | bytes 5242880 | tf_op jit(solution)/shard_map/all_to_all | solution.py:70
  546.2 12.6 %slice-start = ((s8[5242880]{0:T(1024)(128)(4,1)}), s8[1048576]{0:T(1024)(128)(4,1)S(1)}, s32[]{:S(2)}) async-start(s8[5242880]{0:T(1024)(128)(4,1)} %bitcast.517), calls=%async_computation.10 | async-start | bytes 2097152
  553.5 6.5 %copy-start.1 = (f32[1,2,64,40,128]{4,3,2,1,0:T(8,128)S(1)}, f32[1,2,64,40,128]{4,3,2,1,0:T(8,128)}, u32[]{:S(2)}) copy-start(f32[1,2,64,40,128]{4,3,2,1,0:T(8,128)} %param.5) | copy-start | bytes 7864324
  553.5 6.8 %copy-start.2 = (f32[1,2560,128]{2,1,0:T(8,128)S(1)}, f32[1,2560,128]{2,1,0:T(8,128)}, u32[]{:S(2)}) copy-start(f32[1,2560,128]{2,1,0:T(8,128)} %copy.158) | copy-start | bytes 3932164
  553.5 7.1 %copy-start.3 = (f32[1,2560,128]{2,1,0:T(8,128)S(1)}, f32[1,2560,128]{2,1,0:T(8,128)}, u32[]{:S(2)}) copy-start(f32[1,2560,128]{2,1,0:T(8,128)} %copy.141) | copy-start | bytes 3932164
  553.5 7.5 %copy-start.4 = (f32[1,2560,128]{2,1,0:T(8,128)S(1)}, f32[1,2560,128]{2,1,0:T(8,128)}, u32[]{:S(2)}) copy-start(f32[1,2560,128]{2,1,0:T(8,128)} %copy.142) | copy-start | bytes 3932164
  553.5 7.9 %copy-start.5 = (f32[1,2560,128]{2,1,0:T(8,128)S(1)}, f32[1,2560,128]{2,1,0:T(8,128)}, u32[]{:S(2)}) copy-start(f32[1,2560,128]{2,1,0:T(8,128)} %copy.149) | copy-start | bytes 3932164
  553.5 8.2 %copy-start.6 = (f32[1,2560,128]{2,1,0:T(8,128)S(1)}, f32[1,2560,128]{2,1,0:T(8,128)}, u32[]{:S(2)}) copy-start(f32[1,2560,128]{2,1,0:T(8,128)} %copy.150) | copy-start | bytes 3932164
  564.5 14.2 %collective-permute-start = (f32[24,40,128]{2,1,0:T(8,128)S(1)}, f32[24,40,128]{2,1,0:T(8,128)S(1)}, u32[]{:S(2)}, u32[]{:S(2)}) collective-permute-start(f32[24,40,128]{2,1,0:T(8,128)S(1)} %get-tuple-element.46), channel_id=1, source_target_pairs={{0,8},{8,0},{16,24},{24,16},{1,9},{9,1},{17,25},{25,17},{2,10},{10... | collective-permute-start | bytes 1474568 | tf_op jit(solution)/shard_map/ppermute | solution.py:172
  566.1 14.1 %collective-permute-start.2 = (f32[24,40,128]{2,1,0:T(8,128)S(1)}, f32[24,40,128]{2,1,0:T(8,128)S(1)}, u32[]{:S(2)}, u32[]{:S(2)}) collective-permute-start(f32[24,40,128]{2,1,0:T(8,128)S(1)} %get-tuple-element.47), channel_id=1, source_target_pairs={{0,16},{8,24},{16,0},{24,8},{1,17},{9,25},{17,1},{25,9},{2,18},{10... | collective-permute-start | bytes 1474568 | tf_op jit(solution)/shard_map/ppermute | solution.py:172
  568.5 13.9 %collective-permute-start.4 = (f32[8,40,128]{2,1,0:T(8,128)S(1)}, f32[8,40,128]{2,1,0:T(8,128)S(1)}, u32[]{:S(2)}, u32[]{:S(2)}) collective-permute-start(f32[8,40,128]{2,1,0:T(8,128)S(1)} %get-tuple-element.54), channel_id=1, source_target_pairs={{0,8},{8,0},{16,24},{24,16},{1,9},{9,1},{17,25},{25,17},{2,10},{10... | collective-permute-start | bytes 491528 | tf_op jit(solution)/shard_map/ppermute | solution.py:172
  569.1 14.6 %collective-permute-start.6 = (f32[8,40,128]{2,1,0:T(8,128)S(1)}, f32[8,40,128]{2,1,0:T(8,128)S(1)}, u32[]{:S(2)}, u32[]{:S(2)}) collective-permute-start(f32[8,40,128]{2,1,0:T(8,128)S(1)} %get-tuple-element.55), channel_id=1, source_target_pairs={{0,16},{8,24},{16,0},{24,8},{1,17},{9,25},{17,1},{25,9},{2,18},{10... | collective-permute-start | bytes 491528 | tf_op jit(solution)/shard_map/ppermute | solution.py:172
  580.3 22.4 %collective-permute-start.1 = (f32[24,40,128]{2,1,0:T(8,128)S(1)}, f32[24,40,128]{2,1,0:T(8,128)}, u32[]{:S(2)}, u32[]{:S(2)}) collective-permute-start(f32[24,40,128]{2,1,0:T(8,128)S(1)} %get-tuple-element.44), channel_id=1, source_target_pairs={{0,16},{8,24},{16,0},{24,8},{1,17},{9,25},{17,1},{25,9},{2,18},{10... | collective-permute-start | bytes 1474568 | tf_op jit(solution)/shard_map/ppermute | solution.py:172
  581.9 21.9 %collective-permute-start.3 = (f32[24,40,128]{2,1,0:T(8,128)S(1)}, f32[24,40,128]{2,1,0:T(8,128)}, u32[]{:S(2)}, u32[]{:S(2)}) collective-permute-start(f32[24,40,128]{2,1,0:T(8,128)S(1)} %get-tuple-element.45), channel_id=1, source_target_pairs={{0,8},{8,0},{16,24},{24,16},{1,9},{9,1},{17,25},{25,17},{2,10},{10... | collective-permute-start | bytes 1474568 | tf_op jit(solution)/shard_map/ppermute | solution.py:172
  584.4 15.1 %collective-permute-start.5 = (f32[8,40,128]{2,1,0:T(8,128)}, f32[8,40,128]{2,1,0:T(8,128)}, u32[]{:S(2)}, u32[]{:S(2)}) collective-permute-start(f32[8,40,128]{2,1,0:T(8,128)} %get-tuple-element.52), channel_id=1, source_target_pairs={{0,16},{8,24},{16,0},{24,8},{1,17},{9,25},{17,1},{25,9},{2,18},{10... | collective-permute-start | bytes 491528 | tf_op jit(solution)/shard_map/ppermute | solution.py:172
  585.9 14.7 %collective-permute-start.7 = (f32[8,40,128]{2,1,0:T(8,128)S(1)}, f32[8,40,128]{2,1,0:T(8,128)}, u32[]{:S(2)}, u32[]{:S(2)}) collective-permute-start(f32[8,40,128]{2,1,0:T(8,128)S(1)} %get-tuple-element.53), channel_id=1, source_target_pairs={{0,8},{8,0},{16,24},{24,16},{1,9},{9,1},{17,25},{25,17},{2,10},{10... | collective-permute-start | bytes 491528 | tf_op jit(solution)/shard_map/ppermute | solution.py:172
  (26 other events, 82.8 us)

commit v2 on v1

--- a/solution.py
+++ b/solution.py
@@ -50,6 +50,9 @@
     every_axis = ("contrast", "pa", "pb")
     members_total = lax.axis_size("contrast") * groups_pa * groups_pb
 
+    cut = x_rows - x_rows // 4
+    halves = ((0, cut), (cut, x_rows - cut))
+
     def sensitivity(coil_index):
         return (
             coil_maps[coil_index, 0].astype(jnp.float32),
@@ -67,7 +70,7 @@
         return lax.all_to_all(transformed, ("pa", "pb"), split_axis=2, concat_axis=0, tiled=True)
 
     def exchange_back(sendable):
-        return lax.all_to_all(sendable, ("pa", "pb"), split_axis=0, concat_axis=2, tiled=True)[0]
+        return lax.all_to_all(sendable, ("pa", "pb"), split_axis=0, concat_axis=sendable.ndim - 2, tiled=True)[0]
 
     def fourier(portion, coil_index):
         blocks = portion.reshape(groups_pa, groups_pb, 2, depth_share, x_rows, y_rows)
@@ -79,10 +82,13 @@
         misfit_part = jnp.sum(kspace_residual * kspace_residual)
         one_partial_value = contract("czlk,ckfax->afzlx", kspace_residual, inverse_x)
         spatial = contract("afzlx,fldey->aedzxy", one_partial_value, inverse_y)
-        return (
-            spatial.reshape(groups_pa * groups_pb, 2, depth_share, plane_size),
-            misfit_part,
-        )
+        pieces = [
+            spatial[..., first_row : first_row + rows, :].reshape(
+                groups_pa * groups_pb, 2, depth_share, rows * y_rows
+            )
+            for first_row, rows in halves
+        ]
+        return pieces, misfit_part
 
     def recover(received, coil_index, first_row, rows):
         image_part = contract("ckm,ckdz->dmz", received, inverse_z)
@@ -95,9 +101,6 @@
             sens_re * image_part[1] - sens_im * image_part[0],
         )
 
-    cut = x_rows - x_rows // 4
-    halves = ((0, cut), (cut, x_rows - cut))
-    last = coil_total - 1
     arrivals = {}
     outgoing = {}
     returned = {}
@@ -108,7 +111,7 @@
         if kind == "forward":
             arrivals[coil_index] = exchange_forward(sent[coil_index])
         else:
-            returned[coil_index] = exchange_back(outgoing[coil_index])
+            returned[coil_index] = exchange_back(outgoing[coil_index][0])
         if kind == "forward":
             outgoing[coil_index], misfit_parts[coil_index] = fourier(
                 arrivals[coil_index], coil_index
@@ -119,24 +122,18 @@
         scalar_block, every_axis, split_axis=0, concat_axis=0, tiled=True
     )
     misfit_sum = jnp.sum(gathered[:, 0])
-    final = []
-    for first_row, rows in halves:
-        piece = outgoing[last][..., first_row * y_rows : (first_row + rows) * y_rows]
-        final.append(exchange_back(piece))
-    total_re = pixels[0]
-    total_im = pixels[1]
-    for coil_index in range(last):
-        one_re, one_im = recover(returned[coil_index], coil_index, 0, x_rows)
-        total_re = total_re - step_size * one_re
-        total_im = total_im - step_size * one_im
-    total_re, total_im = lax.optimization_barrier((total_re, total_im))
+    bundle = jnp.stack([outgoing[coil_index][1] for coil_index in range(coil_total)], axis=1)
+    remainder = exchange_back(bundle)
+    received = (returned, remainder)
     results = []
-    for (first_row, rows), piece in zip(halves, final):
-        one_re, one_im = recover(piece, last, first_row, rows)
-        moved_re = total_re[first_row : first_row + rows] - step_size * one_re
-        moved_im = total_im[first_row : first_row + rows] - step_size * one_im
+    for part_index, (first_row, rows) in enumerate(halves):
+        moved_re = pixels[0, first_row : first_row + rows]
+        moved_im = pixels[1, first_row : first_row + rows]
+        for coil_index in range(coil_total):
+            one_re, one_im = recover(received[part_index][coil_index], coil_index, first_row, rows)
+            moved_re = moved_re - step_size * one_re
+            moved_im = moved_im - step_size * one_im
         energy = present * (moved_re * moved_re + moved_im * moved_im)
-        moved_re, moved_im, energy = lax.optimization_barrier((moved_re, moved_im, energy))
         energy_total = sum_contrasts(energy)
         norm_value = jnp.sqrt(energy_total)
         factor = jnp.maximum(norm_value - threshold, 0.0) / jnp.maximum(norm_value, threshold)
@@ -154,8 +151,7 @@
     for coil_index in range(coil_total):
         if coil_index + 2 < coil_total:
             steps.append(("forward", coil_index + 2))
-        if coil_index < coil_total - 1:
-            steps.append(("back", coil_index))
+        steps.append(("back", coil_index))
     return steps
 
 

time: 619 us -> 621 us (level)
  waiting for transfers between devices: 229 us -> 190 us
  local copies, waits for them, and re-layouts: 172 us -> 206 us
  other arithmetic: 32.4 us -> 40.6 us
    slice x2 -> x17, local copies, waits for them, and re-layouts: 4.95 us -> 65.4 us  [the longest x12 60.1 us: fourier(): spatial[..., first_row:first_row + rows, :]]
    all_to_all x5, waiting for transfers between devices: 58.5 us -> 9.67 us  [exchange_back(): lax.all_to_all(sendable, ('pa', 'pb'), split_axis=0, concat_axis=sendable...]
    transpose x4 -> x0, local copies, waits for them, and re-layouts: 31.7 us -> none  [contract(): jnp.einsum(pattern, operand, table, precision=lax.Precision.HIGH, preferr...]
    mul x2, other arithmetic: 1.24 us -> 11.3 us  [per_device(): energy = present * (moved_re * moved_re + moved_im * moved_im)]
    slice x5 -> x16, local copies, waits for them, and re-layouts: 9.58 us -> 19.4 us  [recover(): image_part[0]]
    another operation x0 -> x5, local copies, waits for them, and re-layouts: none -> 8.48 us  [per_device(): jnp.stack([outgoing[coil_index][1] for coil_index in range(coil_total)],...]
    reshape x4, local copies, waits for them, and re-layouts: 32.4 us -> 24.8 us  [fourier(): spatial[..., first_row:first_row + rows, :]]
    dot_general x25 -> x28, matrix products: 109 us -> 106 us  [contract(): jnp.einsum(pattern, operand, table, precision=lax.Precision.HIGH, preferr...]
  transfers between devices with their start and end apart: 17 -> 17, of which waited for: 11 -> 9; matrix products, arithmetic and copies ran while one was open for 45% -> 55% of each run, Pallas kernels for 0% -> 0%
where the time goes in v2:
time: 621 us; the launch traced here: 611 us
  local copies, waits for them, and re-layouts  206 us (33%)
  waiting for transfers between devices  190 us (31%)
  matrix products  106 us (17%)
  starting transfers between devices  53.8 us (9%)
  other arithmetic  40.6 us (7%)
  blocking collectives  8.89 us (1%)
  between operations  6.56 us (1%)
    all_to_all x4, waiting for transfers between devices, exchange_forward(): lax.all_to_all(transformed, ('pa', 'pb'), split_axis=2, concat_axis=0, ti...  164 us
    dot_general x28, matrix products, contract(): jnp.einsum(pattern, operand, table, precision=lax.Precision.HIGH, preferr...  106 us
    slice x12, local copies, waits for them, and re-layouts, fourier(): spatial[..., first_row:first_row + rows, :]  60.1 us
    reshape x4, local copies, waits for them, and re-layouts, fourier(): portion.reshape(groups_pa, groups_pb, 2, depth_share, x_rows, y_rows)  35.8 us
    all_to_all x5, starting transfers between devices, exchange_back(): lax.all_to_all(sendable, ('pa', 'pb'), split_axis=0, concat_axis=sendable...  25.4 us
    reshape x4, local copies, waits for them, and re-layouts, fourier(): spatial[..., first_row:first_row + rows, :]  24.8 us
    slice x16, local copies, waits for them, and re-layouts, recover(): image_part[0]  19.4 us
    all_to_all x4, starting transfers between devices, exchange_forward(): lax.all_to_all(transformed, ('pa', 'pb'), split_axis=2, concat_axis=0, ti...  19 us
  transfers between devices with their start and end apart: 17, of which 9 were waited for; matrix products, arithmetic and copies ran while one was open for 55% of the time, Pallas kernels for 0%

profile of v2, /device:TPU:0, one launch (start us, length us, event | category | flops | bytes accessed | tf_op | source)
XLA Modules:
  0.0 611.0 jit_solution(1804075423225272103)
XLA Ops:
  1.4 5.1 multiply_subtract_fusion.3
  11.6 6.6 %all-to-all-start.2 = ((f32[1,2,128,2560]{3,1,0,2:T(2,128)}), f32[1,2,128,2560]{3,1,0,2:T(2,128)}, u32[]{:S(2)}, u32[]{:S(2)}) async-start(f32[1,2,128,2560]{3,1,0,2:T(2,128)} %copy.202), calls=%async_computation.2 | async-start | bytes 5242880 | tf_op jit(solution)/shard_map/all_to_all | solution.py:70
  18.2 4.8 multiply_add_fusion.3
  28.0 50.0 %all-to-all-done.2 = f32[1,2,128,2560]{3,1,0,2:T(2,128)} async-done(((f32[1,2,128,2560]{3,1,0,2:T(2,128)}), f32[1,2,128,2560]{3,1,0,2:T(2,128)}, u32[]{:S(2)}, u32[]{:S(2)}) %all-to-all-start.2) | async-done | bytes 2621472 | tf_op jit(solution)/shard_map/all_to_all | solution.py:70
  78.0 4.2 all-to-all-start.4
  88.6 53.1 %all-to-all-done.4 = f32[1,2,128,2560]{3,1,0,2:T(2,128)S(1)} async-done(((f32[1,2,128,2560]{3,1,0,2:T(2,128)}), f32[1,2,128,2560]{3,1,0,2:T(2,128)S(1)}, u32[]{:S(2)}, u32[]{:S(2)}) %all-to-all-start.4) | async-done | bytes 2621472 | tf_op jit(solution)/shard_map/all_to_all | solution.py:70
  153.4 53.1 %all-to-all-done.6 = f32[1,2,128,2560]{3,1,0,2:T(2,128)S(1)} async-done(((f32[1,2,128,2560]{3,1,0,2:T(2,128)}), f32[1,2,128,2560]{3,1,0,2:T(2,128)S(1)}, u32[]{:S(2)}, u32[]{:S(2)}) %all-to-all-start.6) | async-done | bytes 2621472 | tf_op jit(solution)/shard_map/all_to_all | solution.py:70
  208.0 4.6 all-to-all-start
  220.8 9.0 %reshape.853 = f32[2,4,2,16,64,40]{5,4,3,2,1,0:T(8,128)} reshape(f32[8,1,2,16,2560]{4,3,2,0,1:T(8,128)} %bitcast.636) | data formatting | bytes 5242880 | tf_op jit(solution)/shard_map/reshape | solution.py:76
  229.7 9.1 %fusion.4 = f32[2,160,2,16,64,1,1]{1,4,6,5,0,2,3:T(8,128)S(1)} fusion(f32[1,4,40,1,160]{4,2,1,0,3:T(8,128)S(1)} %get-tuple-element.65, f32[1,4,40,1,160]{4,2,1,0,3:T(8,128)S(1)} %get-tuple-element.64, f32[1,4,40,1,160]{4,2,1,0,3:T(8,128)S(1)} %get-tuple-element.63, f32[2,4,2,16,64,40]{5,4,3,2,1,0:T(8,128)} %reshape.853), kind=kOutput, calls=%fused_computation.4 | convolution fusion | flops 1258598400 | bytes 5550080 | tf_op jit(solution)/shard_map/aeczxy,ceyfl->afzxl/dot_general | solution.py:25
  238.8 5.5 multiply_reduce_fusion.2
  246.3 6.0 fusion.47
  252.4 6.4 %copy.206 = f32[2,4,2,16,48,40]{5,4,3,2,1,0:T(8,128)} copy(f32[2,4,2,16,48,40]{4,5,3,0,1,2:T(8,128)} %bitcast.622) | data formatting | bytes 3932160 | tf_op jit(solution)/shard_map/slice | solution.py:86
  258.8 6.2 %reshape.854 = f32[8,2,16,1920]{3,2,1,0:T(8,128)} reshape(f32[2,4,2,16,48,40]{5,4,3,2,1,0:T(8,128)} %copy.206) | data formatting | bytes 3932160 | tf_op jit(solution)/shard_map/reshape | solution.py:86
  265.0 7.3 %all-to-all-done = f32[1,2,128,2560]{3,1,0,2:T(2,128)} async-done(((f32[1,2,128,2560]{3,1,0,2:T(2,128)}), f32[1,2,128,2560]{3,1,0,2:T(2,128)}, u32[]{:S(2)}, u32[]{:S(2)}) %all-to-all-start) | async-done | bytes 2621472 | tf_op jit(solution)/shard_map/all_to_all | solution.py:70
  272.3 4.7 all-to-all-start.3
  280.8 8.9 %reshape.855 = f32[2,4,2,16,64,40]{5,4,3,2,1,0:T(8,128)} reshape(f32[8,1,2,16,2560]{4,3,2,0,1:T(8,128)} %bitcast.637) | data formatting | bytes 5242880 | tf_op jit(solution)/shard_map/reshape | solution.py:76
  289.7 8.8 %fusion.2 = f32[2,160,2,16,64,1,1]{1,4,6,5,0,2,3:T(8,128)S(1)} fusion(f32[1,4,40,1,160]{4,2,1,0,3:T(8,128)S(1)} %get-tuple-element.65, f32[1,4,40,1,160]{4,2,1,0,3:T(8,128)S(1)} %get-tuple-element.64, f32[1,4,40,1,160]{4,2,1,0,3:T(8,128)S(1)} %get-tuple-element.63, f32[2,4,2,16,64,40]{5,4,3,2,1,0:T(8,128)} %reshape.855), kind=kOutput, calls=%fused_computation.2 | convolution fusion | flops 1258598400 | bytes 5550080 | tf_op jit(solution)/shard_map/aeczxy,ceyfl->afzxl/dot_general | solution.py:25
  298.6 5.6 multiply_reduce_fusion.1
  306.1 6.2 %fusion.50 = f32[2,4,2,16,64,40]{4,5,3,0,1,2:T(8,128)} fusion(f32[2,2,64,16,160,1]{4,2,5,0,3,1:T(8,128)S(1)} %fusion.38, f32[1,160,1,4,40]{1,4,0,3,2:T(8,128)S(1)} %get-tuple-element.62, f32[1,160,1,4,40]{1,4,0,3,2:T(8,128)S(1)} %get-tuple-element.61, f32[1,160,1,4,40]{1,4,0,3,2:T(8,128)S(1)} %get-tuple-element.60), kind=kOutput, calls=%fused_computation.72 | convolution fusion | flops 1258598400 | bytes 5550080 | tf_op jit(solution)/shard_map/afzlx,fldey->aedzxy/dot_general | solution.py:25
  312.3 6.4 %copy.214 = f32[2,4,2,16,48,40]{5,4,3,2,1,0:T(8,128)} copy(f32[2,4,2,16,48,40]{4,5,3,0,1,2:T(8,128)} %bitcast.625) | data formatting | bytes 3932160 | tf_op jit(solution)/shard_map/slice | solution.py:86
  318.7 6.2 %reshape.856 = f32[8,2,16,1920]{3,2,1,0:T(8,128)} reshape(f32[2,4,2,16,48,40]{5,4,3,2,1,0:T(8,128)} %copy.214) | data formatting | bytes 3932160 | tf_op jit(solution)/shard_map/reshape | solution.py:86
  325.0 5.3 all-to-all-start.5
  333.9 8.9 %reshape.857 = f32[2,4,2,16,64,40]{5,4,3,2,1,0:T(8,128)} reshape(f32[8,1,2,16,2560]{4,3,2,0,1:T(8,128)} %bitcast.638) | data formatting | bytes 5242880 | tf_op jit(solution)/shard_map/reshape | solution.py:76
  342.8 8.8 %fusion = f32[2,160,2,16,64,1,1]{1,4,6,5,0,2,3:T(8,128)S(1)} fusion(f32[1,4,40,1,160]{4,2,1,0,3:T(8,128)S(1)} %get-tuple-element.65, f32[1,4,40,1,160]{4,2,1,0,3:T(8,128)S(1)} %get-tuple-element.64, f32[1,4,40,1,160]{4,2,1,0,3:T(8,128)S(1)} %get-tuple-element.63, f32[2,4,2,16,64,40]{5,4,3,2,1,0:T(8,128)} %reshape.857), kind=kOutput, calls=%fused_computation | convolution fusion | flops 1258598400 | bytes 5550080 | tf_op jit(solution)/shard_map/aeczxy,ceyfl->afzxl/dot_general | solution.py:25
  351.7 5.5 multiply_reduce_fusion
  359.2 6.5 %fusion.53 = f32[2,4,2,16,64,40]{4,5,3,0,1,2:T(8,128)} fusion(f32[2,2,64,16,160,1]{4,2,5,0,3,1:T(8,128)S(1)} %fusion.36, f32[1,160,1,4,40]{1,4,0,3,2:T(8,128)S(1)} %get-tuple-element.62, f32[1,160,1,4,40]{1,4,0,3,2:T(8,128)S(1)} %get-tuple-element.61, f32[1,160,1,4,40]{1,4,0,3,2:T(8,128)S(1)} %get-tuple-element.60), kind=kOutput, calls=%fused_computation.73 | convolution fusion | flops 1258598400 | bytes 5550080 | tf_op jit(solution)/shard_map/afzlx,fldey->aedzxy/dot_general | solution.py:25
  365.7 6.4 %copy.222 = f32[2,4,2,16,48,40]{5,4,3,2,1,0:T(8,128)} copy(f32[2,4,2,16,48,40]{4,5,3,0,1,2:T(8,128)} %bitcast.628) | data formatting | bytes 3932160 | tf_op jit(solution)/shard_map/slice | solution.py:86
  372.1 6.2 %reshape.858 = f32[8,2,16,1920]{3,2,1,0:T(8,128)} reshape(f32[2,4,2,16,48,40]{5,4,3,2,1,0:T(8,128)} %copy.222) | data formatting | bytes 3932160 | tf_op jit(solution)/shard_map/reshape | solution.py:86
  378.3 5.1 all-to-all-start.7
  387.1 9.0 %reshape.851 = f32[2,4,2,16,64,40]{5,4,3,2,1,0:T(8,128)} reshape(f32[8,1,2,16,2560]{4,3,2,0,1:T(8,128)} %bitcast.639) | data formatting | bytes 5242880 | tf_op jit(solution)/shard_map/reshape | solution.py:76
  396.1 8.8 %fusion.6 = f32[2,160,2,16,64,1,1]{1,4,6,5,0,2,3:T(8,128)S(1)} fusion(f32[1,4,40,1,160]{4,2,1,0,3:T(8,128)S(1)} %get-tuple-element.65, f32[1,4,40,1,160]{4,2,1,0,3:T(8,128)S(1)} %get-tuple-element.64, f32[1,4,40,1,160]{4,2,1,0,3:T(8,128)S(1)} %get-tuple-element.63, f32[2,4,2,16,64,40]{5,4,3,2,1,0:T(8,128)} %reshape.851), kind=kOutput, calls=%fused_computation.6 | convolution fusion | flops 1258598400 | bytes 5550080 | tf_op jit(solution)/shard_map/aeczxy,ceyfl->afzxl/dot_general | solution.py:25
  405.0 5.5 multiply_reduce_fusion.3
  412.4 6.3 %fusion.44 = f32[2,4,2,16,64,40]{4,5,3,0,1,2:T(8,128)} fusion(f32[2,2,64,16,160,1]{4,2,5,0,3,1:T(8,128)S(1)} %fusion.42, f32[1,160,1,4,40]{1,4,0,3,2:T(8,128)S(1)} %get-tuple-element.62, f32[1,160,1,4,40]{1,4,0,3,2:T(8,128)S(1)} %get-tuple-element.61, f32[1,160,1,4,40]{1,4,0,3,2:T(8,128)S(1)} %get-tuple-element.60), kind=kOutput, calls=%fused_computation.70 | convolution fusion | flops 1258598400 | bytes 5550080 | tf_op jit(solution)/shard_map/afzlx,fldey->aedzxy/dot_general | solution.py:25
  418.7 6.4 %copy.198 = f32[2,4,2,16,48,40]{5,4,3,2,1,0:T(8,128)} copy(f32[2,4,2,16,48,40]{4,5,3,0,1,2:T(8,128)} %bitcast.631) | data formatting | bytes 3932160 | tf_op jit(solution)/shard_map/slice | solution.py:86
  425.1 6.2 %reshape.852 = f32[8,2,16,1920]{3,2,1,0:T(8,128)} reshape(f32[2,4,2,16,48,40]{5,4,3,2,1,0:T(8,128)} %copy.198) | data formatting | bytes 3932160 | tf_op jit(solution)/shard_map/reshape | solution.py:86
  431.3 5.2 all-to-all-start.1
  436.5 6.7 %slice_convert_fusion.7 = (f32[1,1,64,40,128]{4,3,2,1,0:T(8,128)}, f32[1,1,64,40,128]{4,3,2,1,0:T(8,128)}, f32[1,1,64,40,128]{4,3,2,1,0:T(8,128)}, f32[1,1,64,40...) fusion(bf16[4,2,64,40,128]{4,3,2,1,0:T(8,128)(2,1)} %param.6), kind=kLoop, calls=%fused_computation.119 | loop fusion | flops 2621440 | bytes 15728640 | tf_op jit(solution)/shard_map/convert_element_type | solution.py:58
  443.2 6.4 %slice.426 = f32[2,4,2,16,16,40]{4,5,3,0,1,2:T(8,128)} slice(f32[2,4,2,16,64,40]{4,5,3,0,1,2:T(8,128)} %fusion.44), slice={[0:2], [0:4], [0:2], [0:16], [48:64], [0:40]} | slice | bytes 1310720 | tf_op jit(solution)/shard_map/slice | solution.py:86
  460.9 4.1 copy.226
  466.1 4.1 copy.229
  478.1 4.3 copy.227
  489.5 5.1 all-to-all-start.8
  518.9 7.7 %add_multiply_fusion = (f32[48,40,128]{2,1,0:T(8,128)S(1)}, f32[48,40,128]{2,1,0:T(8,128)}, f32[48,40,128]{2,1,0:T(8,128)}) fusion(f32[]{:T(128)} %bitcast.9, f32[48,40,128]{2,1,0:T(8,128)} %bitcast.657, f32[1,1,64,40,128]{4,3,2,1,0:T(8,128)} %get-tuple-element.22, f32[48,40,128]{2,1,0:T(8,128)} %bitcast.656, f32[1,1,64,40,128]{4,3,2,1,0:T(8,128)} %get-tuple-element.23, ...), kind=kLoop, calls=%fused_computation.109 | loop fusion | flops 8847360 | bytes 20643844 | tf_op jit(solution)/shard_map/mul | solution.py:136
  529.7 10.6 %collective-permute-done = f32[24,40,128]{2,1,0:T(8,128)S(1)} collective-permute-done((f32[24,40,128]{2,1,0:T(8,128)S(1)}, f32[24,40,128]{2,1,0:T(8,128)S(1)}, u32[]{:S(2)}, u32[]{:S(2)}) %collective-permute-start) | collective-permute-done | bytes 491552 | tf_op jit(solution)/shard_map/ppermute | solution.py:168
  544.7 9.7 %all-to-all-done.8 = f32[8,4,2,16,640]{4,3,2,1,0:T(8,128)} async-done(((f32[8,4,2,16,640]{4,3,2,1,0:T(8,128)}), f32[8,4,2,16,640]{4,3,2,1,0:T(8,128)}, u32[]{:S(2)}, u32[]{:S(2)}) %all-to-all-start.8) | async-done | bytes 2621472 | tf_op jit(solution)/shard_map/all_to_all | solution.py:73
  588.6 8.9 %all_to_all.144 = f32[32,1,128]{2,1,0:T(1,128)S(1)} all-to-all(f32[32,1,128]{2,1,0:T(1,128)S(1)} %broadcast_in_dim.17), channel_id=1, replica_groups=mesh['contrast'=4,'pa'=2,'pb'=4] {'contrast','pa','pb'}, dimensions={0} | all-to-all | bytes 32768 | tf_op jit(solution)/shard_map/all_to_all | solution.py:121
  602.9 4.3 collective-permute-done.5
  (146 shorter events, 154.3 us)
Async XLA Ops:
  11.6 6.6 %copy-start = (f32[1,2,64,40,128]{4,3,2,1,0:T(8,128)S(1)}, f32[1,2,64,40,128]{4,3,2,1,0:T(8,128)}, u32[]{:S(2)}) copy-start(f32[1,2,64,40,128]{4,3,2,1,0:T(8,128)} %param.5) | copy-start | bytes 7864324
  11.6 66.4 %all-to-all-start.2 = ((f32[1,2,128,2560]{3,1,0,2:T(2,128)}), f32[1,2,128,2560]{3,1,0,2:T(2,128)}, u32[]{:S(2)}, u32[]{:S(2)}) async-start(f32[1,2,128,2560]{3,1,0,2:T(2,128)} %copy.202), calls=%async_computation.2 | async-start | bytes 5242880 | tf_op jit(solution)/shard_map/all_to_all | solution.py:70
  18.2 4.8 copy-start.4
  78.0 63.8 %all-to-all-start.4 = ((f32[1,2,128,2560]{3,1,0,2:T(2,128)}), f32[1,2,128,2560]{3,1,0,2:T(2,128)S(1)}, u32[]{:S(2)}, u32[]{:S(2)}) async-start(f32[1,2,128,2560]{3,1,0,2:T(2,128)} %copy.210), calls=%async_computation.4 | async-start | bytes 5242880 | tf_op jit(solution)/shard_map/all_to_all | solution.py:70
  141.8 1.5 copy-start.3
  143.3 63.3 %all-to-all-start.6 = ((f32[1,2,128,2560]{3,1,0,2:T(2,128)}), f32[1,2,128,2560]{3,1,0,2:T(2,128)S(1)}, u32[]{:S(2)}, u32[]{:S(2)}) async-start(f32[1,2,128,2560]{3,1,0,2:T(2,128)} %copy.218), calls=%async_computation.6 | async-start | bytes 5242880 | tf_op jit(solution)/shard_map/all_to_all | solution.py:70
  206.6 1.5 copy-start.2
  208.0 64.3 %all-to-all-start = ((f32[1,2,128,2560]{3,1,0,2:T(2,128)}), f32[1,2,128,2560]{3,1,0,2:T(2,128)}, u32[]{:S(2)}, u32[]{:S(2)}) async-start(f32[1,2,128,2560]{3,1,0,2:T(2,128)} %copy.194), calls=%async_computation | async-start | bytes 5242880 | tf_op jit(solution)/shard_map/all_to_all | solution.py:70
  272.3 52.6 %all-to-all-start.3 = ((f32[8,2,16,1920]{3,2,1,0:T(8,128)}), f32[8,2,16,1920]{3,2,1,0:T(8,128)}, u32[]{:S(2)}, u32[]{:S(2)}) async-start(f32[8,2,16,1920]{3,2,1,0:T(8,128)} %reshape.854), calls=%async_computation.3 | async-start | bytes 3932160 | tf_op jit(solution)/shard_map/all_to_all | solution.py:73
  325.0 53.4 %all-to-all-start.5 = ((f32[8,2,16,1920]{3,2,1,0:T(8,128)}), f32[8,2,16,1920]{3,2,1,0:T(8,128)}, u32[]{:S(2)}, u32[]{:S(2)}) async-start(f32[8,2,16,1920]{3,2,1,0:T(8,128)} %reshape.856), calls=%async_computation.5 | async-start | bytes 3932160 | tf_op jit(solution)/shard_map/all_to_all | solution.py:73
  378.3 53.0 %all-to-all-start.7 = ((f32[8,2,16,1920]{3,2,1,0:T(8,128)}), f32[8,2,16,1920]{3,2,1,0:T(8,128)}, u32[]{:S(2)}, u32[]{:S(2)}) async-start(f32[8,2,16,1920]{3,2,1,0:T(8,128)} %reshape.858), calls=%async_computation.7 | async-start | bytes 3932160 | tf_op jit(solution)/shard_map/all_to_all | solution.py:73
  431.3 18.4 %slice-start.4 = ((s8[5242880]{0:T(1024)(128)(4,1)}), s8[1048576]{0:T(1024)(128)(4,1)S(1)}, s32[]{:S(2)}) async-start(s8[5242880]{0:T(1024)(128)(4,1)} %bitcast.629), calls=%async_computation.14 | async-start | bytes 2097152
  431.3 58.2 %all-to-all-start.1 = ((f32[8,2,16,1920]{3,2,1,0:T(8,128)}), f32[8,2,16,1920]{3,2,1,0:T(8,128)}, u32[]{:S(2)}, u32[]{:S(2)}) async-start(f32[8,2,16,1920]{3,2,1,0:T(8,128)} %reshape.852), calls=%async_computation.1 | async-start | bytes 3932160 | tf_op jit(solution)/shard_map/all_to_all | solution.py:73
  436.5 13.1 %slice-start.5 = ((s8[5242880]{0:T(1024)(128)(4,1)}), s8[4194304]{0:T(1024)(128)(4,1)S(1)}, s32[]{:S(2)}) async-start(s8[5242880]{0:T(1024)(128)(4,1)} %bitcast.629), calls=%async_computation.15 | async-start | bytes 8388608
  436.5 16.8 %slice-start.2 = ((s8[5242880]{0:T(1024)(128)(4,1)}), s8[1048576]{0:T(1024)(128)(4,1)S(1)}, s32[]{:S(2)}) async-start(s8[5242880]{0:T(1024)(128)(4,1)} %bitcast.626), calls=%async_computation.12 | async-start | bytes 2097152
  443.2 10.2 %slice-start.3 = ((s8[5242880]{0:T(1024)(128)(4,1)}), s8[4194304]{0:T(1024)(128)(4,1)S(1)}, s32[]{:S(2)}) async-start(s8[5242880]{0:T(1024)(128)(4,1)} %bitcast.626), calls=%async_computation.13 | async-start | bytes 8388608
  449.6 7.5 %slice-start = ((s8[5242880]{0:T(1024)(128)(4,1)}), s8[4194304]{0:T(1024)(128)(4,1)S(1)}, s32[]{:S(2)}) async-start(s8[5242880]{0:T(1024)(128)(4,1)} %bitcast.623), calls=%async_computation.10 | async-start | bytes 8388608
  453.4 3.8 slice-start.1
  489.5 64.9 %all-to-all-start.8 = ((f32[8,4,2,16,640]{4,3,2,1,0:T(8,128)}), f32[8,4,2,16,640]{4,3,2,1,0:T(8,128)}, u32[]{:S(2)}, u32[]{:S(2)}) async-start(f32[8,4,2,16,640]{4,3,2,1,0:T(8,128)} %copy.230), calls=%async_computation.8 | async-start | bytes 5242880 | tf_op jit(solution)/shard_map/all_to_all | solution.py:73
  513.7 5.2 copy-start.1
  526.7 13.7 %collective-permute-start = (f32[24,40,128]{2,1,0:T(8,128)S(1)}, f32[24,40,128]{2,1,0:T(8,128)S(1)}, u32[]{:S(2)}, u32[]{:S(2)}) collective-permute-start(f32[24,40,128]{2,1,0:T(8,128)S(1)} %get-tuple-element.40), channel_id=1, source_target_pairs={{0,8},{8,0},{16,24},{24,16},{1,9},{9,1},{17,25},{25,17},{2,10},{10... | collective-permute-start | bytes 1474568 | tf_op jit(solution)/shard_map/ppermute | solution.py:168
  528.2 13.4 %collective-permute-start.2 = (f32[24,40,128]{2,1,0:T(8,128)S(1)}, f32[24,40,128]{2,1,0:T(8,128)S(1)}, u32[]{:S(2)}, u32[]{:S(2)}) collective-permute-start(f32[24,40,128]{2,1,0:T(8,128)S(1)} %get-tuple-element.41), channel_id=1, source_target_pairs={{0,16},{8,24},{16,0},{24,8},{1,17},{9,25},{17,1},{25,9},{2,18},{10... | collective-permute-start | bytes 1474568 | tf_op jit(solution)/shard_map/ppermute | solution.py:168
  542.7 56.0 %collective-permute-start.1 = (f32[24,40,128]{2,1,0:T(8,128)}, f32[24,40,128]{2,1,0:T(8,128)}, u32[]{:S(2)}, u32[]{:S(2)}) collective-permute-start(f32[24,40,128]{2,1,0:T(8,128)} %get-tuple-element.38), channel_id=1, source_target_pairs={{0,16},{8,24},{16,0},{24,8},{1,17},{9,25},{17,1},{25,9},{2,18},{10... | collective-permute-start | bytes 1474568 | tf_op jit(solution)/shard_map/ppermute | solution.py:168
  544.2 55.8 %collective-permute-start.3 = (f32[24,40,128]{2,1,0:T(8,128)}, f32[24,40,128]{2,1,0:T(8,128)}, u32[]{:S(2)}, u32[]{:S(2)}) collective-permute-start(f32[24,40,128]{2,1,0:T(8,128)} %get-tuple-element.39), channel_id=1, source_target_pairs={{0,8},{8,0},{16,24},{24,16},{1,9},{9,1},{17,25},{25,17},{2,10},{10... | collective-permute-start | bytes 1474568 | tf_op jit(solution)/shard_map/ppermute | solution.py:168
  575.2 4.1 copy-start.7
  582.9 19.5 %copy-start.5 = (f32[48,40,128]{2,1,0:T(8,128)S(1)}, f32[48,40,128]{2,1,0:T(8,128)}, u32[]{:S(2)}) copy-start(f32[48,40,128]{2,1,0:T(8,128)} %get-tuple-element.3) | copy-start | bytes 2949124
  582.9 19.5 %copy-start.6 = (f32[48,40,128]{2,1,0:T(8,128)S(1)}, f32[48,40,128]{2,1,0:T(8,128)}, u32[]{:S(2)}) copy-start(f32[48,40,128]{2,1,0:T(8,128)} %get-tuple-element.4) | copy-start | bytes 2949124
  583.0 18.2 %collective-permute-start.4 = (f32[8,40,128]{2,1,0:T(8,128)S(1)}, f32[8,40,128]{2,1,0:T(8,128)S(1)}, u32[]{:S(2)}, u32[]{:S(2)}) collective-permute-start(f32[8,40,128]{2,1,0:T(8,128)S(1)} %get-tuple-element.54), channel_id=1, source_target_pairs={{0,8},{8,0},{16,24},{24,16},{1,9},{9,1},{17,25},{25,17},{2,10},{10... | collective-permute-start | bytes 491528 | tf_op jit(solution)/shard_map/ppermute | solution.py:168
  584.5 16.7 %collective-permute-start.6 = (f32[8,40,128]{2,1,0:T(8,128)S(1)}, f32[8,40,128]{2,1,0:T(8,128)S(1)}, u32[]{:S(2)}, u32[]{:S(2)}) collective-permute-start(f32[8,40,128]{2,1,0:T(8,128)S(1)} %get-tuple-element.55), channel_id=1, source_target_pairs={{0,16},{8,24},{16,0},{24,8},{1,17},{9,25},{17,1},{25,9},{2,18},{10... | collective-permute-start | bytes 491528 | tf_op jit(solution)/shard_map/ppermute | solution.py:168
  601.3 5.9 collective-permute-start.5
  601.9 5.6 collective-permute-start.7
  602.4 5.1 copy-start.8
  602.4 5.1 copy-start.9

commit v3 on v1

--- a/solution.py
+++ b/solution.py
@@ -79,10 +79,8 @@
         misfit_part = jnp.sum(kspace_residual * kspace_residual)
         one_partial_value = contract("czlk,ckfax->afzlx", kspace_residual, inverse_x)
         spatial = contract("afzlx,fldey->aedzxy", one_partial_value, inverse_y)
-        return (
-            spatial.reshape(groups_pa * groups_pb, 2, depth_share, plane_size),
-            misfit_part,
-        )
+        packed = spatial.reshape(groups_pa * groups_pb, 2, depth_share, plane_size)
+        return packed, misfit_part
 
     def recover(received, coil_index, first_row, rows):
         image_part = contract("ckm,ckdz->dmz", received, inverse_z)
@@ -95,7 +93,7 @@
             sens_re * image_part[1] - sens_im * image_part[0],
         )
 
-    cut = x_rows - x_rows // 4
+    cut = x_rows - x_rows * 3 // 8
     halves = ((0, cut), (cut, x_rows - cut))
     last = coil_total - 1
     arrivals = {}

time: 619 us -> 625 us (level)
  blocking collectives: 9.27 us -> 0 us
    all_to_all x5, waiting for transfers between devices: 58.5 us -> 68.4 us  [exchange_back(): lax.all_to_all(sendable, ('pa', 'pb'), split_axis=0, concat_axis=2, tiled...]
    all_to_all x1 -> x0, blocking collectives: 9.27 us -> none  [per_device(): lax.all_to_all(scalar_block, every_axis, split_axis=0, concat_axis=0, til...]
    slice x10 -> x8, local copies, waits for them, and re-layouts: 15.8 us -> 15.7 us  [recover(): image_part[1]]
  transfers between devices with their start and end apart: 17 -> 18, of which waited for: 11 -> 11; matrix products, arithmetic and copies ran while one was open for 45% -> 45% of each run, Pallas kernels for 0% -> 0%
where the time goes in v3:
time: 625 us; the launch traced here: 614 us
  waiting for transfers between devices  235 us (38%)
  local copies, waits for them, and re-layouts  174 us (28%)
  matrix products  110 us (18%)
  starting transfers between devices  54.3 us (9%)
  other arithmetic  34.8 us (6%)
  between operations  6.83 us (1%)
    all_to_all x4, waiting for transfers between devices, exchange_forward(): lax.all_to_all(transformed, ('pa', 'pb'), split_axis=2, concat_axis=0, ti...  158 us
    dot_general x25, matrix products, contract(): jnp.einsum(pattern, operand, table, precision=lax.Precision.HIGH, preferr...  110 us
    all_to_all x5, waiting for transfers between devices, exchange_back(): lax.all_to_all(sendable, ('pa', 'pb'), split_axis=0, concat_axis=2, tiled...  68.4 us
    reshape x4, local copies, waits for them, and re-layouts, fourier(): portion.reshape(groups_pa, groups_pb, 2, depth_share, x_rows, y_rows)  36 us
    reshape x4, local copies, waits for them, and re-layouts, fourier(): packed = spatial.reshape(groups_pa * groups_pb, 2, depth_share, plane_size)  32.5 us
    transpose x4, local copies, waits for them, and re-layouts, contract(): jnp.einsum(pattern, operand, table, precision=lax.Precision.HIGH, preferr...  31.9 us
    all_to_all x5, starting transfers between devices, exchange_back(): lax.all_to_all(sendable, ('pa', 'pb'), split_axis=0, concat_axis=2, tiled...  22.2 us
    all_to_all x4, starting transfers between devices, exchange_forward(): lax.all_to_all(transformed, ('pa', 'pb'), split_axis=2, concat_axis=0, ti...  19.5 us
  transfers between devices with their start and end apart: 18, of which 11 were waited for; matrix products, arithmetic and copies ran while one was open for 45% of the time, Pallas kernels for 0%

profile of v3, /device:TPU:0, one launch (start us, length us, event | category | flops | bytes accessed | tf_op | source)
XLA Modules:
  0.0 614.5 jit_solution(8740244217397124607)
XLA Ops:
  1.4 4.7 fusion.92
  11.1 6.6 %all-to-all-start.4 = ((f32[1,2,128,2560]{3,1,0,2:T(2,128)}), f32[1,2,128,2560]{3,1,0,2:T(2,128)}, u32[]{:S(2)}, u32[]{:S(2)}) async-start(f32[1,2,128,2560]{3,1,0,2:T(2,128)} %copy.141), calls=%async_computation.4 | async-start | bytes 5242880 | tf_op jit(solution)/shard_map/all_to_all | solution.py:67
  17.7 3.9 fusion.88
  26.5 51.0 %all-to-all-done.4 = f32[1,2,128,2560]{3,1,0,2:T(2,128)} async-done(((f32[1,2,128,2560]{3,1,0,2:T(2,128)}), f32[1,2,128,2560]{3,1,0,2:T(2,128)}, u32[]{:S(2)}, u32[]{:S(2)}) %all-to-all-start.4) | async-done | bytes 2621472 | tf_op jit(solution)/shard_map/all_to_all | solution.py:67
  77.5 3.8 all-to-all-start
  87.9 53.1 %all-to-all-done = f32[1,2,128,2560]{3,1,0,2:T(2,128)S(1)} async-done(((f32[1,2,128,2560]{3,1,0,2:T(2,128)}), f32[1,2,128,2560]{3,1,0,2:T(2,128)S(1)}, u32[]{:S(2)}, u32[]{:S(2)}) %all-to-all-start) | async-done | bytes 2621472 | tf_op jit(solution)/shard_map/all_to_all | solution.py:67
  142.5 4.4 all-to-all-start.6
  153.5 53.2 %all-to-all-done.6 = f32[1,2,128,2560]{3,1,0,2:T(2,128)} async-done(((f32[1,2,128,2560]{3,1,0,2:T(2,128)}), f32[1,2,128,2560]{3,1,0,2:T(2,128)}, u32[]{:S(2)}, u32[]{:S(2)}) %all-to-all-start.6) | async-done | bytes 2621472 | tf_op jit(solution)/shard_map/all_to_all | solution.py:67
  206.7 4.7 all-to-all-start.2
  215.9 3.7 copy.244
  219.6 9.0 %reshape.828 = f32[2,4,2,16,64,40]{5,4,3,2,1,0:T(8,128)} reshape(f32[8,1,2,16,2560]{4,3,2,0,1:T(8,128)} %bitcast.535) | data formatting | bytes 5242880 | tf_op jit(solution)/shard_map/reshape | solution.py:73
  228.6 9.3 %fusion = f32[2,160,2,16,64,1,1]{1,4,6,5,0,2,3:T(8,128)S(1)} fusion(f32[1,4,40,1,160]{4,2,1,0,3:T(8,128)S(1)} %get-tuple-element.65, f32[1,4,40,1,160]{4,2,1,0,3:T(8,128)S(1)} %get-tuple-element.64, f32[1,4,40,1,160]{4,2,1,0,3:T(8,128)S(1)} %get-tuple-element.63, f32[2,4,2,16,64,40]{5,4,3,2,1,0:T(8,128)} %reshape.828), kind=kOutput, calls=%fused_computation | convolution fusion | flops 1258598400 | bytes 5550080 | tf_op jit(solution)/shard_map/aeczxy,ceyfl->afzxl/dot_general | solution.py:25
  238.0 5.5 multiply_reduce_fusion
  245.5 6.1 fusion.53
  251.5 8.0 %copy.153 = f32[2,4,2,16,64,40]{5,4,3,2,1,0:T(8,128)} copy(f32[2,4,2,16,64,40]{4,5,3,0,1,2:T(8,128)} %fusion.53) | data formatting | bytes 5242880 | tf_op jit(solution)/shard_map/afzlx,fldey->aedzxy/transpose | solution.py:25
  259.5 8.1 %reshape.829 = f32[8,2,16,2560]{3,2,1,0:T(8,128)} reshape(f32[2,4,2,16,64,40]{5,4,3,2,1,0:T(8,128)} %copy.153) | data formatting | bytes 5242880 | tf_op jit(solution)/shard_map/reshape | solution.py:82
  271.1 4.1 all-to-all-start.8
  278.0 23.2 %all-to-all-done.8 = f32[8,2,16,960]{3,2,1,0:T(8,128)S(1)} async-done(((f32[8,2,16,960]{3,2,1,0:T(8,128)}), f32[8,2,16,960]{3,2,1,0:T(8,128)S(1)}, u32[]{:S(2)}, u32[]{:S(2)}) %all-to-all-start.8) | async-done | bytes 983072 | tf_op jit(solution)/shard_map/all_to_all | solution.py:70
  302.3 3.8 all-to-all-start.7
  306.0 3.7 copy.245
  309.7 9.0 %reshape.826 = f32[2,4,2,16,64,40]{5,4,3,2,1,0:T(8,128)} reshape(f32[8,1,2,16,2560]{4,3,2,0,1:T(8,128)} %bitcast.536) | data formatting | bytes 5242880 | tf_op jit(solution)/shard_map/reshape | solution.py:73
  318.7 10.1 %fusion.2 = f32[2,160,2,16,64,1,1]{1,4,6,5,0,2,3:T(8,128)S(1)} fusion(f32[1,4,40,1,160]{4,2,1,0,3:T(8,128)} %copy-done.47, f32[1,4,40,1,160]{4,2,1,0,3:T(8,128)} %copy-done.46, f32[1,4,40,1,160]{4,2,1,0,3:T(8,128)} %copy-done.45, f32[2,4,2,16,64,40]{5,4,3,2,1,0:T(8,128)} %reshape.826), kind=kOutput, calls=%fused_computation.2 | convolution fusion | flops 1258598400 | bytes 5550080 | tf_op jit(solution)/shard_map/aeczxy,ceyfl->afzxl/dot_general | solution.py:25
  328.9 5.6 multiply_reduce_fusion.1
  336.5 6.1 fusion.50
  342.5 8.0 %copy.145 = f32[2,4,2,16,64,40]{5,4,3,2,1,0:T(8,128)} copy(f32[2,4,2,16,64,40]{4,5,3,0,1,2:T(8,128)} %fusion.50) | data formatting | bytes 5242880 | tf_op jit(solution)/shard_map/afzlx,fldey->aedzxy/transpose | solution.py:25
  350.5 8.1 %reshape.827 = f32[8,2,16,2560]{3,2,1,0:T(8,128)} reshape(f32[2,4,2,16,64,40]{5,4,3,2,1,0:T(8,128)} %copy.145) | data formatting | bytes 5242880 | tf_op jit(solution)/shard_map/reshape | solution.py:82
  358.6 5.5 all-to-all-start.5
  364.1 3.7 copy.247
  367.8 9.0 %reshape.822 = f32[2,4,2,16,64,40]{5,4,3,2,1,0:T(8,128)} reshape(f32[8,1,2,16,2560]{4,3,2,0,1:T(8,128)} %bitcast.537) | data formatting | bytes 5242880 | tf_op jit(solution)/shard_map/reshape | solution.py:73
  376.8 10.1 %fusion.6 = f32[2,160,2,16,64,1,1]{1,4,6,5,0,2,3:T(8,128)S(1)} fusion(f32[1,4,40,1,160]{4,2,1,0,3:T(8,128)} %copy-done.47, f32[1,4,40,1,160]{4,2,1,0,3:T(8,128)} %copy-done.46, f32[1,4,40,1,160]{4,2,1,0,3:T(8,128)} %copy-done.45, f32[2,4,2,16,64,40]{5,4,3,2,1,0:T(8,128)} %reshape.822), kind=kOutput, calls=%fused_computation.6 | convolution fusion | flops 1258598400 | bytes 5550080 | tf_op jit(solution)/shard_map/aeczxy,ceyfl->afzxl/dot_general | solution.py:25
  386.9 5.6 multiply_reduce_fusion.3
  394.5 6.2 %fusion.44 = f32[2,4,2,16,64,40]{4,5,3,0,1,2:T(8,128)} fusion(f32[2,2,64,16,160,1]{4,2,5,0,3,1:T(8,128)S(1)} %fusion.42, f32[1,160,1,4,40]{1,4,0,3,2:T(8,128)S(1)} %copy-done.18, f32[1,160,1,4,40]{1,4,0,3,2:T(8,128)S(1)} %copy-done.14, f32[1,160,1,4,40]{1,4,0,3,2:T(8,128)S(1)} %get-tuple-element.60), kind=kOutput, calls=%fused_computation.69 | convolution fusion | flops 1258598400 | bytes 5550080 | tf_op jit(solution)/shard_map/afzlx,fldey->aedzxy/dot_general | solution.py:25
  400.7 8.0 %copy.129 = f32[2,4,2,16,64,40]{5,4,3,2,1,0:T(8,128)} copy(f32[2,4,2,16,64,40]{4,5,3,0,1,2:T(8,128)} %fusion.44) | data formatting | bytes 5242880 | tf_op jit(solution)/shard_map/afzlx,fldey->aedzxy/transpose | solution.py:25
  408.7 8.2 %reshape.823 = f32[8,2,16,2560]{3,2,1,0:T(8,128)} reshape(f32[2,4,2,16,64,40]{5,4,3,2,1,0:T(8,128)} %copy.129) | data formatting | bytes 5242880 | tf_op jit(solution)/shard_map/reshape | solution.py:82
  416.9 7.0 %all-to-all-done.5 = f32[8,2,16,2560]{3,2,1,0:T(8,128)} async-done(((f32[8,2,16,2560]{3,2,1,0:T(8,128)}), f32[8,2,16,2560]{3,2,1,0:T(8,128)}, u32[]{:S(2)}, u32[]{:S(2)}) %all-to-all-start.5) | async-done | bytes 2621472 | tf_op jit(solution)/shard_map/all_to_all | solution.py:70
  423.8 4.4 all-to-all-start.1
  428.2 3.7 copy.246
  431.9 9.0 %reshape.824 = f32[2,4,2,16,64,40]{5,4,3,2,1,0:T(8,128)} reshape(f32[8,1,2,16,2560]{4,3,2,0,1:T(8,128)} %bitcast.538) | data formatting | bytes 5242880 | tf_op jit(solution)/shard_map/reshape | solution.py:73
  440.9 10.1 %fusion.4 = f32[2,160,2,16,64,1,1]{1,4,6,5,0,2,3:T(8,128)S(1)} fusion(f32[1,4,40,1,160]{4,2,1,0,3:T(8,128)} %copy-done.47, f32[1,4,40,1,160]{4,2,1,0,3:T(8,128)} %copy-done.46, f32[1,4,40,1,160]{4,2,1,0,3:T(8,128)} %copy-done.45, f32[2,4,2,16,64,40]{5,4,3,2,1,0:T(8,128)} %reshape.824), kind=kOutput, calls=%fused_computation.4 | convolution fusion | flops 1258598400 | bytes 5550080 | tf_op jit(solution)/shard_map/aeczxy,ceyfl->afzxl/dot_general | solution.py:25
  451.1 5.6 multiply_reduce_fusion.2
  458.7 6.3 %fusion.47 = f32[2,4,2,16,64,40]{4,5,3,0,1,2:T(8,128)} fusion(f32[2,2,64,16,160,1]{4,2,5,0,3,1:T(8,128)S(1)} %fusion.40, f32[1,160,1,4,40]{1,4,0,3,2:T(8,128)S(1)} %copy-done.19, f32[1,160,1,4,40]{1,4,0,3,2:T(8,128)S(1)} %copy-done.15, f32[1,160,1,4,40]{1,4,0,3,2:T(8,128)S(1)} %get-tuple-element.60), kind=kOutput, calls=%fused_computation.70 | convolution fusion | flops 1258598400 | bytes 5550080 | tf_op jit(solution)/shard_map/afzlx,fldey->aedzxy/dot_general | solution.py:25
  465.0 8.0 %copy.137 = f32[2,4,2,16,64,40]{5,4,3,2,1,0:T(8,128)} copy(f32[2,4,2,16,64,40]{4,5,3,0,1,2:T(8,128)} %fusion.47) | data formatting | bytes 5242880 | tf_op jit(solution)/shard_map/afzlx,fldey->aedzxy/transpose | solution.py:25
  472.9 8.1 %reshape.825 = f32[8,2,16,2560]{3,2,1,0:T(8,128)} reshape(f32[2,4,2,16,64,40]{5,4,3,2,1,0:T(8,128)} %copy.137) | data formatting | bytes 5242880 | tf_op jit(solution)/shard_map/reshape | solution.py:82
  481.1 6.9 %all-to-all-done.1 = f32[8,2,16,2560]{3,2,1,0:T(8,128)} async-done(((f32[8,2,16,2560]{3,2,1,0:T(8,128)}), f32[8,2,16,2560]{3,2,1,0:T(8,128)}, u32[]{:S(2)}, u32[]{:S(2)}) %all-to-all-start.1) | async-done | bytes 2621472 | tf_op jit(solution)/shard_map/all_to_all | solution.py:70
  488.0 4.4 all-to-all-start.3
  520.8 31.3 %all-to-all-done.3 = f32[8,2,16,2560]{3,2,1,0:T(8,128)} async-done(((f32[8,2,16,2560]{3,2,1,0:T(8,128)}), f32[8,2,16,2560]{3,2,1,0:T(8,128)}, u32[]{:S(2)}, u32[]{:S(2)}) %all-to-all-start.3) | async-done | bytes 2621472 | tf_op jit(solution)/shard_map/all_to_all | solution.py:70
  562.8 5.3 fusion.79
  603.6 5.2 collective-permute-done.1
  (183 shorter events, 119.6 us)
Async XLA Ops:
  11.1 6.6 %copy-start = (f32[1,2,64,40,128]{4,3,2,1,0:T(8,128)S(1)}, f32[1,2,64,40,128]{4,3,2,1,0:T(8,128)}, u32[]{:S(2)}) copy-start(f32[1,2,64,40,128]{4,3,2,1,0:T(8,128)} %param.5) | copy-start | bytes 7864324
  11.1 66.4 %all-to-all-start.4 = ((f32[1,2,128,2560]{3,1,0,2:T(2,128)}), f32[1,2,128,2560]{3,1,0,2:T(2,128)}, u32[]{:S(2)}, u32[]{:S(2)}) async-start(f32[1,2,128,2560]{3,1,0,2:T(2,128)} %copy.141), calls=%async_computation.4 | async-start | bytes 5242880 | tf_op jit(solution)/shard_map/all_to_all | solution.py:67
  77.5 63.5 %all-to-all-start = ((f32[1,2,128,2560]{3,1,0,2:T(2,128)}), f32[1,2,128,2560]{3,1,0,2:T(2,128)S(1)}, u32[]{:S(2)}, u32[]{:S(2)}) async-start(f32[1,2,128,2560]{3,1,0,2:T(2,128)} %copy.125), calls=%async_computation | async-start | bytes 5242880 | tf_op jit(solution)/shard_map/all_to_all | solution.py:67
  142.5 64.1 %all-to-all-start.6 = ((f32[1,2,128,2560]{3,1,0,2:T(2,128)}), f32[1,2,128,2560]{3,1,0,2:T(2,128)}, u32[]{:S(2)}, u32[]{:S(2)}) async-start(f32[1,2,128,2560]{3,1,0,2:T(2,128)} %copy.149), calls=%async_computation.6 | async-start | bytes 5242880 | tf_op jit(solution)/shard_map/all_to_all | solution.py:67
  206.7 64.4 %all-to-all-start.2 = ((f32[1,2,128,2560]{3,1,0,2:T(2,128)}), f32[1,2,128,2560]{3,1,0,2:T(2,128)}, u32[]{:S(2)}, u32[]{:S(2)}) async-start(f32[1,2,128,2560]{3,1,0,2:T(2,128)} %copy.133), calls=%async_computation.2 | async-start | bytes 5242880 | tf_op jit(solution)/shard_map/all_to_all | solution.py:67
  212.4 25.6 %copy-start.33 = (f32[1,2,64,1,128]{4,2,0,1,3:T(8,128)}, f32[1,2,64,1,128]{4,2,0,1,3:T(8,128)S(1)}, u32[]{:S(2)}) copy-start(f32[1,2,64,1,128]{4,2,0,1,3:T(8,128)S(1)} %get-tuple-element.69) | copy-start | bytes 196612
  212.4 25.6 %copy-start.37 = (f32[1,2,64,1,128]{4,2,0,1,3:T(8,128)}, f32[1,2,64,1,128]{4,2,0,1,3:T(8,128)S(1)}, u32[]{:S(2)}) copy-start(f32[1,2,64,1,128]{4,2,0,1,3:T(8,128)S(1)} %get-tuple-element.70) | copy-start | bytes 196612
  212.4 25.6 %copy-start.41 = (f32[1,2,64,1,128]{4,2,0,1,3:T(8,128)}, f32[1,2,64,1,128]{4,2,0,1,3:T(8,128)S(1)}, u32[]{:S(2)}) copy-start(f32[1,2,64,1,128]{4,2,0,1,3:T(8,128)S(1)} %get-tuple-element.71) | copy-start | bytes 196612
  212.7 30.7 %copy-start.25 = (f32[1,128,1,2,64]{1,4,0,2,3:T(8,128)}, f32[1,128,1,2,64]{1,4,0,2,3:T(8,128)S(1)}, u32[]{:S(2)}) copy-start(f32[1,128,1,2,64]{1,4,0,2,3:T(8,128)S(1)} %get-tuple-element.67) | copy-start | bytes 196612
  212.8 30.7 %copy-start.29 = (f32[1,128,1,2,64]{1,4,0,2,3:T(8,128)}, f32[1,128,1,2,64]{1,4,0,2,3:T(8,128)S(1)}, u32[]{:S(2)}) copy-start(f32[1,128,1,2,64]{1,4,0,2,3:T(8,128)S(1)} %get-tuple-element.68) | copy-start | bytes 196612
  213.5 15.1 %copy-start.45 = (f32[1,4,40,1,160]{4,2,1,0,3:T(8,128)}, f32[1,4,40,1,160]{4,2,1,0,3:T(8,128)S(1)}, u32[]{:S(2)}) copy-start(f32[1,4,40,1,160]{4,2,1,0,3:T(8,128)S(1)} %get-tuple-element.63) | copy-start | bytes 307204
  213.5 15.1 %copy-start.46 = (f32[1,4,40,1,160]{4,2,1,0,3:T(8,128)}, f32[1,4,40,1,160]{4,2,1,0,3:T(8,128)S(1)}, u32[]{:S(2)}) copy-start(f32[1,4,40,1,160]{4,2,1,0,3:T(8,128)S(1)} %get-tuple-element.64) | copy-start | bytes 307204
  213.5 15.1 %copy-start.47 = (f32[1,4,40,1,160]{4,2,1,0,3:T(8,128)}, f32[1,4,40,1,160]{4,2,1,0,3:T(8,128)S(1)}, u32[]{:S(2)}) copy-start(f32[1,4,40,1,160]{4,2,1,0,3:T(8,128)S(1)} %get-tuple-element.65) | copy-start | bytes 307204
  214.3 31.2 %copy-start.12 = (f32[1,160,1,4,40]{1,4,0,3,2:T(8,128)}, f32[1,160,1,4,40]{1,4,0,3,2:T(8,128)S(1)}, u32[]{:S(2)}) copy-start(f32[1,160,1,4,40]{1,4,0,3,2:T(8,128)S(1)} %get-tuple-element.61) | copy-start | bytes 307204
  214.3 31.2 %copy-start.16 = (f32[1,160,1,4,40]{1,4,0,3,2:T(8,128)}, f32[1,160,1,4,40]{1,4,0,3,2:T(8,128)S(1)}, u32[]{:S(2)}) copy-start(f32[1,160,1,4,40]{1,4,0,3,2:T(8,128)S(1)} %get-tuple-element.62) | copy-start | bytes 307204
  271.1 30.1 %all-to-all-start.8 = ((f32[8,2,16,960]{3,2,1,0:T(8,128)}), f32[8,2,16,960]{3,2,1,0:T(8,128)S(1)}, u32[]{:S(2)}, u32[]{:S(2)}) async-start(f32[8,2,16,960]{3,2,1,0:T(8,128)} %slice.232), calls=%async_computation.8 | async-start | bytes 2097152 | tf_op jit(solution)/shard_map/all_to_all | solution.py:70
  302.3 56.3 %all-to-all-start.7 = ((f32[8,2,16,1600]{3,2,1,0:T(8,128)}), f32[8,2,16,1600]{3,2,1,0:T(8,128)S(1)}, u32[]{:S(2)}, u32[]{:S(2)}) async-start(f32[8,2,16,1600]{3,2,1,0:T(8,128)} %slice.227), calls=%async_computation.7 | async-start | bytes 3407872 | tf_op jit(solution)/shard_map/all_to_all | solution.py:70
  318.7 10.1 %copy-start.34 = (f32[1,2,64,1,128]{4,2,0,1,3:T(8,128)S(1)}, f32[1,2,64,1,128]{4,2,0,1,3:T(8,128)}, u32[]{:S(2)}) copy-start(f32[1,2,64,1,128]{4,2,0,1,3:T(8,128)} %copy-done.33) | copy-start | bytes 196612
  318.7 10.1 %copy-start.38 = (f32[1,2,64,1,128]{4,2,0,1,3:T(8,128)S(1)}, f32[1,2,64,1,128]{4,2,0,1,3:T(8,128)}, u32[]{:S(2)}) copy-start(f32[1,2,64,1,128]{4,2,0,1,3:T(8,128)} %copy-done.37) | copy-start | bytes 196612
  318.7 10.1 %copy-start.42 = (f32[1,2,64,1,128]{4,2,0,1,3:T(8,128)S(1)}, f32[1,2,64,1,128]{4,2,0,1,3:T(8,128)}, u32[]{:S(2)}) copy-start(f32[1,2,64,1,128]{4,2,0,1,3:T(8,128)} %copy-done.41) | copy-start | bytes 196612
  358.6 65.2 %all-to-all-start.5 = ((f32[8,2,16,2560]{3,2,1,0:T(8,128)}), f32[8,2,16,2560]{3,2,1,0:T(8,128)}, u32[]{:S(2)}, u32[]{:S(2)}) async-start(f32[8,2,16,2560]{3,2,1,0:T(8,128)} %reshape.827), calls=%async_computation.5 | async-start | bytes 5242880 | tf_op jit(solution)/shard_map/all_to_all | solution.py:70
  376.8 10.1 %copy-start.35 = (f32[1,2,64,1,128]{4,2,0,1,3:T(8,128)S(1)}, f32[1,2,64,1,128]{4,2,0,1,3:T(8,128)}, u32[]{:S(2)}) copy-start(f32[1,2,64,1,128]{4,2,0,1,3:T(8,128)} %copy-done.33) | copy-start | bytes 196612
  376.8 10.1 %copy-start.39 = (f32[1,2,64,1,128]{4,2,0,1,3:T(8,128)S(1)}, f32[1,2,64,1,128]{4,2,0,1,3:T(8,128)}, u32[]{:S(2)}) copy-start(f32[1,2,64,1,128]{4,2,0,1,3:T(8,128)} %copy-done.37) | copy-start | bytes 196612
  376.8 10.1 %copy-start.43 = (f32[1,2,64,1,128]{4,2,0,1,3:T(8,128)S(1)}, f32[1,2,64,1,128]{4,2,0,1,3:T(8,128)}, u32[]{:S(2)}) copy-start(f32[1,2,64,1,128]{4,2,0,1,3:T(8,128)} %copy-done.41) | copy-start | bytes 196612
  423.8 64.1 %all-to-all-start.1 = ((f32[8,2,16,2560]{3,2,1,0:T(8,128)}), f32[8,2,16,2560]{3,2,1,0:T(8,128)}, u32[]{:S(2)}, u32[]{:S(2)}) async-start(f32[8,2,16,2560]{3,2,1,0:T(8,128)} %reshape.823), calls=%async_computation.1 | async-start | bytes 5242880 | tf_op jit(solution)/shard_map/all_to_all | solution.py:70
  440.9 10.1 %copy-start.36 = (f32[1,2,64,1,128]{4,2,0,1,3:T(8,128)S(1)}, f32[1,2,64,1,128]{4,2,0,1,3:T(8,128)}, u32[]{:S(2)}) copy-start(f32[1,2,64,1,128]{4,2,0,1,3:T(8,128)} %copy-done.33) | copy-start | bytes 196612
  440.9 10.1 %copy-start.40 = (f32[1,2,64,1,128]{4,2,0,1,3:T(8,128)S(1)}, f32[1,2,64,1,128]{4,2,0,1,3:T(8,128)}, u32[]{:S(2)}) copy-start(f32[1,2,64,1,128]{4,2,0,1,3:T(8,128)} %copy-done.37) | copy-start | bytes 196612
  440.9 10.1 %copy-start.44 = (f32[1,2,64,1,128]{4,2,0,1,3:T(8,128)S(1)}, f32[1,2,64,1,128]{4,2,0,1,3:T(8,128)}, u32[]{:S(2)}) copy-start(f32[1,2,64,1,128]{4,2,0,1,3:T(8,128)} %copy-done.41) | copy-start | bytes 196612
  451.1 5.6 copy-start.28
  451.1 5.6 copy-start.32
  488.0 64.1 %all-to-all-start.3 = ((f32[8,2,16,2560]{3,2,1,0:T(8,128)}), f32[8,2,16,2560]{3,2,1,0:T(8,128)}, u32[]{:S(2)}, u32[]{:S(2)}) async-start(f32[8,2,16,2560]{3,2,1,0:T(8,128)} %reshape.825), calls=%async_computation.3 | async-start | bytes 5242880 | tf_op jit(solution)/shard_map/all_to_all | solution.py:70
  555.5 12.5 %slice-start = ((s8[5242880]{0:T(1024)(128)(4,1)}), s8[1048576]{0:T(1024)(128)(4,1)S(1)}, s32[]{:S(2)}) async-start(s8[5242880]{0:T(1024)(128)(4,1)} %bitcast.517), calls=%async_computation.10 | async-start | bytes 2097152
  562.7 6.5 %copy-start.1 = (f32[1,2,64,40,128]{4,3,2,1,0:T(8,128)S(1)}, f32[1,2,64,40,128]{4,3,2,1,0:T(8,128)}, u32[]{:S(2)}) copy-start(f32[1,2,64,40,128]{4,3,2,1,0:T(8,128)} %param.5) | copy-start | bytes 7864324
  562.7 6.8 %copy-start.2 = (f32[1,2560,128]{2,1,0:T(8,128)S(1)}, f32[1,2560,128]{2,1,0:T(8,128)}, u32[]{:S(2)}) copy-start(f32[1,2560,128]{2,1,0:T(8,128)} %copy.148) | copy-start | bytes 3932164
  562.7 7.1 %copy-start.3 = (f32[1,2560,128]{2,1,0:T(8,128)S(1)}, f32[1,2560,128]{2,1,0:T(8,128)}, u32[]{:S(2)}) copy-start(f32[1,2560,128]{2,1,0:T(8,128)} %copy.131) | copy-start | bytes 3932164
  562.7 7.5 %copy-start.4 = (f32[1,2560,128]{2,1,0:T(8,128)S(1)}, f32[1,2560,128]{2,1,0:T(8,128)}, u32[]{:S(2)}) copy-start(f32[1,2560,128]{2,1,0:T(8,128)} %copy.132) | copy-start | bytes 3932164
  562.7 7.9 %copy-start.5 = (f32[1,2560,128]{2,1,0:T(8,128)S(1)}, f32[1,2560,128]{2,1,0:T(8,128)}, u32[]{:S(2)}) copy-start(f32[1,2560,128]{2,1,0:T(8,128)} %copy.139) | copy-start | bytes 3932164
  562.7 8.2 %copy-start.6 = (f32[1,2560,128]{2,1,0:T(8,128)S(1)}, f32[1,2560,128]{2,1,0:T(8,128)}, u32[]{:S(2)}) copy-start(f32[1,2560,128]{2,1,0:T(8,128)} %copy.140) | copy-start | bytes 3932164
  576.1 11.5 %collective-permute-start.4 = (f32[12,40,128]{2,1,0:T(8,128)}, f32[12,40,128]{2,1,0:T(8,128)}, u32[]{:S(2)}, u32[]{:S(2)}) collective-permute-start(f32[12,40,128]{2,1,0:T(8,128)} %get-tuple-element.54), channel_id=1, source_target_pairs={{0,8},{8,0},{16,24},{24,16},{1,9},{9,1},{17,25},{25,17},{2,10},{10... | collective-permute-start | bytes 737288 | tf_op jit(solution)/shard_map/ppermute | solution.py:170
  577.6 10.0 %collective-permute-start.6 = (f32[12,40,128]{2,1,0:T(8,128)}, f32[12,40,128]{2,1,0:T(8,128)}, u32[]{:S(2)}, u32[]{:S(2)}) collective-permute-start(f32[12,40,128]{2,1,0:T(8,128)} %get-tuple-element.55), channel_id=1, source_target_pairs={{0,16},{8,24},{16,0},{24,8},{1,17},{9,25},{17,1},{25,9},{2,18},{10... | collective-permute-start | bytes 737288 | tf_op jit(solution)/shard_map/ppermute | solution.py:170
  580.1 13.5 %collective-permute-start = (f32[20,40,128]{2,1,0:T(8,128)}, f32[20,40,128]{2,1,0:T(8,128)}, u32[]{:S(2)}, u32[]{:S(2)}) collective-permute-start(f32[20,40,128]{2,1,0:T(8,128)} %get-tuple-element.48), channel_id=1, source_target_pairs={{0,8},{8,0},{16,24},{24,16},{1,9},{9,1},{17,25},{25,17},{2,10},{10... | collective-permute-start | bytes 1228808 | tf_op jit(solution)/shard_map/ppermute | solution.py:170
  580.6 15.1 %collective-permute-start.2 = (f32[20,40,128]{2,1,0:T(8,128)}, f32[20,40,128]{2,1,0:T(8,128)}, u32[]{:S(2)}, u32[]{:S(2)}) collective-permute-start(f32[20,40,128]{2,1,0:T(8,128)} %get-tuple-element.49), channel_id=1, source_target_pairs={{0,16},{8,24},{16,0},{24,8},{1,17},{9,25},{17,1},{25,9},{2,18},{10... | collective-permute-start | bytes 1228808 | tf_op jit(solution)/shard_map/ppermute | solution.py:170
  584.4 15.5 %all-to-all-start.9 = ((f32[32,1,128]{2,1,0:T(1,128)}), f32[32,1,128]{2,1,0:T(1,128)S(1)}, u32[]{:S(2)}, u32[]{:S(2)}) async-start(f32[32,1,128]{2,1,0:T(1,128)} %broadcast_in_dim.17), calls=%async_computation.9 | async-start | bytes 32768 | tf_op jit(solution)/shard_map/all_to_all | solution.py:116
  589.5 13.8 %copy-start.22 = (f32[24,40,128]{2,1,0:T(8,128)S(1)}, f32[24,40,128]{2,1,0:T(8,128)}, u32[]{:S(2)}) copy-start(f32[24,40,128]{2,1,0:T(8,128)} %get-tuple-element.15) | copy-start | bytes 1474564
  589.5 11.6 %collective-permute-start.5 = (f32[12,40,128]{2,1,0:T(8,128)}, f32[12,40,128]{2,1,0:T(8,128)}, u32[]{:S(2)}, u32[]{:S(2)}) collective-permute-start(f32[12,40,128]{2,1,0:T(8,128)} %get-tuple-element.52), channel_id=1, source_target_pairs={{0,16},{8,24},{16,0},{24,8},{1,17},{9,25},{17,1},{25,9},{2,18},{10... | collective-permute-start | bytes 737288 | tf_op jit(solution)/shard_map/ppermute | solution.py:170
  591.3 10.9 %collective-permute-start.7 = (f32[12,40,128]{2,1,0:T(8,128)}, f32[12,40,128]{2,1,0:T(8,128)}, u32[]{:S(2)}, u32[]{:S(2)}) collective-permute-start(f32[12,40,128]{2,1,0:T(8,128)} %get-tuple-element.53), channel_id=1, source_target_pairs={{0,8},{8,0},{16,24},{24,16},{1,9},{9,1},{17,25},{25,17},{2,10},{10... | collective-permute-start | bytes 737288 | tf_op jit(solution)/shard_map/ppermute | solution.py:170
  597.8 11.0 %collective-permute-start.1 = (f32[20,40,128]{2,1,0:T(8,128)}, f32[20,40,128]{2,1,0:T(8,128)S(1)}, u32[]{:S(2)}, u32[]{:S(2)}) collective-permute-start(f32[20,40,128]{2,1,0:T(8,128)} %get-tuple-element.46), channel_id=1, source_target_pairs={{0,16},{8,24},{16,0},{24,8},{1,17},{9,25},{17,1},{25,9},{2,18},{10... | collective-permute-start | bytes 1228808 | tf_op jit(solution)/shard_map/ppermute | solution.py:170
  599.3 10.5 %collective-permute-start.3 = (f32[20,40,128]{2,1,0:T(8,128)}, f32[20,40,128]{2,1,0:T(8,128)S(1)}, u32[]{:S(2)}, u32[]{:S(2)}) collective-permute-start(f32[20,40,128]{2,1,0:T(8,128)} %get-tuple-element.47), channel_id=1, source_target_pairs={{0,8},{8,0},{16,24},{24,16},{1,9},{9,1},{17,25},{25,17},{2,10},{10... | collective-permute-start | bytes 1228808 | tf_op jit(solution)/shard_map/ppermute | solution.py:170
  (20 other events, 54.9 us)
